TPU v7x, 32 devices: a whole 2x2x4 slice. The times are simulated.
32 devices in a mesh: row: 8 (over y, x, core), col: 4 (over z).
Axes of the slice: x: 2, y: 2, z: 4, core: 2. Of those that a mesh axis runs over, the one named last changes fastest.
Arguments:
- contact_map: bfloat16 [512, 512, 128], P('row', 'col'), may hold values from -6 to 6
- conv_weight: bfloat16 [2, 3, 3, 3, 128, 128], replicated, may hold values from -0.1875 to 0.1875
- conv_bias: float32 [2, 3, 128], replicated, may hold values from -0.5 to 0.5
Outputs:
- trunk_out: bfloat16 [512, 512, 128], P('row', 'col')
All inputs are finite; a program needn't handle non-finite values.
Results may differ from a plain program's by a relative error of at most 0.0085.
Values may be sent and summed in bfloat16 or wider, within the bound.
A program may use at most 128 MiB of HBM per device.

v0:
```python
import jax
import jax.numpy as jnp
from jax import lax
from jax.sharding import PartitionSpec as P


def with_halo(array, sides, width):
    for axis, dim in sides:
        devices, length = (lax.axis_size(axis), array.shape[dim])
        up = [(i, (i + 1) % devices) for i in range(devices - 1)]
        down = [(j, i) for i, j in up]
        last = lax.slice_in_dim(array, length - width, length, axis=dim)
        initial = lax.slice_in_dim(array, 0, width, axis=dim)
        before = lax.ppermute(last, axis, up)
        after = lax.ppermute(initial, axis, down)
        array = jnp.concatenate([before, array, after], axis=dim)
    return array


def convolve(padded, kernel, rows, cols, dilation):
    total = jnp.zeros((rows, cols, kernel.shape[3]), jnp.float32)
    for tap_row in range(3):
        for tap_col in range(3):
            piece = padded[
                tap_row * dilation : tap_row * dilation + rows,
                tap_col * dilation : tap_col * dilation + cols,
            ]
            total = total + jnp.dot(
                piece, kernel[tap_row, tap_col], preferred_element_type=jnp.float32
            )
    return total


def average(current, flipped):
    return ((current.astype(jnp.float32) + flipped.astype(jnp.float32)) * 0.5).astype(jnp.bfloat16)


def strip_pad(hidden, dilation):
    widened = jnp.pad(hidden, ((0, 0), (dilation, dilation), (0, 0)))
    return with_halo(widened, ((("row", "col"), 0),), dilation)


def run_block(current, flipped, conv_weight, conv_bias, block, padder):
    rows, cols = (current.shape[0], current.shape[1])
    mirrored = average(current, flipped)
    hidden = mirrored
    result = mirrored
    for layer, dilation in enumerate((1, 2, 4)):
        padded = padder(hidden, dilation)
        total = (
            convolve(padded, conv_weight[block, layer], rows, cols, dilation)
            + conv_bias[block, layer]
        )
        if layer < 2:
            hidden = jax.nn.relu(total).astype(jnp.bfloat16)
        else:
            result = (mirrored.astype(jnp.float32) + total).astype(jnp.bfloat16)
    return result


def per_device(contact_map, conv_weight, conv_bias):
    blocks = conv_weight.shape[0]
    current = lax.all_to_all(contact_map, "col", split_axis=0, concat_axis=1, tiled=True)
    for block in range(blocks):
        columns = lax.all_to_all(current, ("row", "col"), split_axis=1, concat_axis=0, tiled=True)
        flipped = jnp.transpose(columns, (1, 0, 2))
        current = run_block(current, flipped, conv_weight, conv_bias, block, strip_pad)
    return lax.all_to_all(current, "col", split_axis=1, concat_axis=0, tiled=True)


def solution(mesh):
    in_specs = (P("row", "col", None), P(), P())
    out_specs = P("row", "col", None)
    return jax.shard_map(
        per_device, mesh=mesh, in_specs=in_specs, out_specs=out_specs, check_vma=False
    )
```

profile of v0, /device:TPU:12, one launch (start us, length us, event | category | flops | bytes accessed | tf_op | source)
XLA Modules:
  0.0 501.4 jit_solution(15225654004325715221)
XLA Ops:
  0.0 51.7 %all_to_all.54 = bf16[64,128,128]{2,1,0:T(8,128)(2,1)S(1)} all-to-all(bf16[64,128,128]{2,1,0:T(8,128)(2,1)} %param.3), channel_id=1, replica_groups=mesh['row'=8,'col'=4] {'col'}, dimensions={0} | all-to-all | bytes 4194304 | tf_op jit(solution)/shard_map/all_to_all | solution.py:63
  51.8 2.7 copy.9
  54.5 5.4 %all-to-all-start.1 = ((bf16[16,512,128]{2,0,1:T(8,128)(2,1)}), bf16[16,512,128]{2,0,1:T(8,128)(2,1)}, u32[]{:S(2)}, u32[]{:S(2)}) async-start(bf16[16,512,128]{2,0,1:T(8,128)(2,1)} %copy.9), calls=%async_computation.1 | async-start | bytes 4194304 | tf_op jit(solution)/shard_map/all_to_all | solution.py:65
  62.8 45.1 %all-to-all-done.1 = bf16[16,512,128]{2,0,1:T(8,128)(2,1)} async-done(((bf16[16,512,128]{2,0,1:T(8,128)(2,1)}), bf16[16,512,128]{2,0,1:T(8,128)(2,1)}, u32[]{:S(2)}, u32[]{:S(2)}) %all-to-all-start.1) | async-done | bytes 2097184 | tf_op jit(solution)/shard_map/all_to_all | solution.py:65
  118.9 2.7 fusion.128
  121.6 4.2 collective-permute-start
  126.4 2.7 fusion.65
  129.1 2.7 fusion.68
  131.8 2.7 fusion.74
  134.4 2.7 fusion.71
  137.1 2.7 fusion.104
  139.8 11.9 %maximum_convert_fusion.3 = bf16[16,512,128]{2,1,0:T(8,128)(2,1)S(1)} fusion(f32[16,512,128]{2,1,0:T(8,128)} %fusion.65, f32[16,512,128]{2,1,0:T(8,128)} %fusion.68, f32[16,512,128]{2,1,0:T(8,128)} %fusion.128, f32[16,512,128]{2,1,0:T(8,128)} %fusion.145, f32[16,512,128]{2,1,0:T(8,128)} %fusion.130, f32[16,512,128]{2,1,0:T(8,128)} %fusion.104, ...), kind=kOutput, calls=%fused_computation.11 | convolution fusion | flops 284164096 | bytes 37947904 | tf_op jit(solution)/shard_map/dot_general | solution.py:28
  160.6 4.9 collective-permute-start.3
  165.5 2.7 fusion.124
  168.2 8.3 %collective-permute-done.3 = bf16[2,516,128]{2,1,0:T(8,128)(2,1)S(1)} collective-permute-done((bf16[2,516,128]{2,1,0:T(8,128)(2,1)S(1)}, bf16[2,516,128]{2,1,0:T(8,128)(2,1)S(1)}, u32[]{:S(2)}, u32[]{:S(2)}) %collective-permute-start.3) | collective-permute-done | bytes 264224 | tf_op jit(solution)/shard_map/ppermute | solution.py:15
  176.6 2.7 fusion.17
  179.2 2.7 fusion.20
  181.9 2.7 fusion.26
  184.6 2.7 fusion.23
  187.3 2.7 fusion.98
  190.0 11.9 %maximum_convert_fusion.2 = bf16[16,512,128]{2,1,0:T(8,128)(2,1)S(1)} fusion(f32[16,512,128]{2,1,0:T(8,128)} %fusion.17, f32[16,512,128]{2,1,0:T(8,128)} %fusion.20, f32[16,512,128]{2,1,0:T(8,128)} %fusion.124, f32[16,512,128]{2,1,0:T(8,128)} %fusion.144, f32[16,512,128]{2,1,0:T(8,128)} %fusion.126, f32[16,512,128]{2,1,0:T(8,128)} %fusion.98, ...), kind=kOutput, calls=%fused_computation.10 | convolution fusion | flops 284164096 | bytes 38081024 | tf_op jit(solution)/shard_map/dot_general | solution.py:28
  202.2 2.9 collective-permute-start.5
  205.2 2.7 fusion.122
  207.8 2.7 fusion.120
  211.1 3.1 collective-permute-start.4
  218.9 2.7 fusion.41
  221.5 2.7 fusion.44
  224.2 4.7 collective-permute-done.4
  228.9 2.7 fusion.50
  231.6 2.7 fusion.47
  234.2 2.7 fusion.94
  236.9 11.8 %add_convert_fusion.1 = bf16[16,512,128]{2,1,0:T(8,128)(2,1)S(1)} fusion(f32[16,512,128]{2,1,0:T(8,128)} %fusion.41, f32[16,512,128]{2,1,0:T(8,128)} %fusion.44, f32[16,512,128]{2,1,0:T(8,128)} %fusion.120, f32[16,512,128]{2,1,0:T(8,128)} %fusion.143, f32[16,512,128]{2,1,0:T(8,128)} %fusion.122, f32[16,512,128]{2,1,0:T(8,128)} %fusion.94, ...), kind=kOutput, calls=%fused_computation.9 | convolution fusion | flops 285212672 | bytes 40444416 | tf_op jit(solution)/shard_map/dot_general | solution.py:28
  250.1 57.0 %all_to_all.55 = bf16[16,512,128]{2,0,1:T(8,128)(2,1)S(1)} all-to-all(bf16[16,512,128]{2,0,1:T(8,128)(2,1)S(1)} %copy.11), channel_id=1, replica_groups=mesh['row'=8,'col'=4] {'row','col'}, dimensions={1} | all-to-all | bytes 4194304 | tf_op jit(solution)/shard_map/all_to_all | solution.py:65
  308.2 2.7 fusion.118
  315.4 2.7 fusion.116
  318.7 4.1 collective-permute-start.6
  322.9 2.7 fusion.53
  325.5 2.7 fusion.56
  328.2 2.7 fusion.62
  330.9 2.7 fusion.59
  333.6 2.7 fusion.88
  336.3 11.9 %maximum_convert_fusion.1 = bf16[16,512,128]{2,1,0:T(8,128)(2,1)S(1)} fusion(f32[16,512,128]{2,1,0:T(8,128)} %fusion.53, f32[16,512,128]{2,1,0:T(8,128)} %fusion.56, f32[16,512,128]{2,1,0:T(8,128)} %fusion.116, f32[16,512,128]{2,1,0:T(8,128)} %fusion.142, f32[16,512,128]{2,1,0:T(8,128)} %fusion.118, f32[16,512,128]{2,1,0:T(8,128)} %fusion.88, ...), kind=kOutput, calls=%fused_computation.8 | convolution fusion | flops 284164096 | bytes 37947904 | tf_op jit(solution)/shard_map/dot_general | solution.py:28
  348.9 2.7 fusion.114
  356.8 5.5 %collective-permute-start.9 = (bf16[2,516,128]{2,1,0:T(8,128)(2,1)S(1)}, bf16[2,516,128]{2,1,0:T(8,128)(2,1)S(1)}, u32[]{:S(2)}, u32[]{:S(2)}) collective-permute-start(bf16[2,516,128]{2,1,0:T(8,128)(2,1)S(1)} %get-tuple-element.12), channel_id=1, source_target_pairs={{1,0},{2,1},{3,2},{4,3},{5,4},{6,5},{7,6},{8,7},{9,8},{10,9},{11,1... | collective-permute-start | bytes 792584 | tf_op jit(solution)/shard_map/ppermute | solution.py:15
  362.3 2.7 fusion.112
  365.0 8.6 %collective-permute-done.9 = bf16[2,516,128]{2,1,0:T(8,128)(2,1)S(1)} collective-permute-done((bf16[2,516,128]{2,1,0:T(8,128)(2,1)S(1)}, bf16[2,516,128]{2,1,0:T(8,128)(2,1)S(1)}, u32[]{:S(2)}, u32[]{:S(2)}) %collective-permute-start.9) | collective-permute-done | bytes 264224 | tf_op jit(solution)/shard_map/ppermute | solution.py:15
  373.6 2.7 fusion.5
  376.3 2.7 fusion.8
  379.0 2.7 fusion.14
  381.7 2.7 fusion.11
  384.3 2.7 fusion.82
  387.1 11.9 %maximum_convert_fusion = bf16[16,512,128]{2,1,0:T(8,128)(2,1)S(1)} fusion(f32[16,512,128]{2,1,0:T(8,128)} %fusion.5, f32[16,512,128]{2,1,0:T(8,128)} %fusion.8, f32[16,512,128]{2,1,0:T(8,128)} %fusion.112, f32[16,512,128]{2,1,0:T(8,128)} %fusion.141, f32[16,512,128]{2,1,0:T(8,128)} %fusion.114, f32[16,512,128]{2,1,0:T(8,128)} %fusion.82, ...), kind=kOutput, calls=%fused_computation.7 | convolution fusion | flops 284164096 | bytes 38081024 | tf_op jit(solution)/shard_map/dot_general | solution.py:28
  399.3 3.3 collective-permute-start.11
  402.6 2.6 fusion.110
  405.3 2.7 fusion.108
  408.5 2.8 collective-permute-start.10
  416.0 2.7 fusion.29
  418.7 2.7 fusion.32
  421.4 5.0 collective-permute-done.10
  426.3 2.7 fusion.38
  429.0 2.7 fusion.35
  431.7 2.7 fusion.78
  434.4 11.8 %add_convert_fusion = bf16[16,512,128]{2,1,0:T(8,128)(2,1)S(1)} fusion(f32[16,512,128]{2,1,0:T(8,128)} %fusion.29, f32[16,512,128]{2,1,0:T(8,128)} %fusion.32, f32[16,512,128]{2,1,0:T(8,128)} %fusion.108, f32[16,512,128]{2,1,0:T(8,128)} %fusion.140, f32[16,512,128]{2,1,0:T(8,128)} %fusion.110, f32[16,512,128]{2,1,0:T(8,128)} %fusion.78, ...), kind=kOutput, calls=%fused_computation.6 | convolution fusion | flops 285212672 | bytes 40444416 | tf_op jit(solution)/shard_map/dot_general | solution.py:28
  447.5 51.5 %all_to_all.56 = bf16[16,512,128]{2,0,1:T(8,128)(2,1)S(1)} all-to-all(bf16[16,512,128]{2,0,1:T(8,128)(2,1)S(1)} %copy.13), channel_id=1, replica_groups=mesh['row'=8,'col'=4] {'col'}, dimensions={1} | all-to-all | bytes 4194304 | tf_op jit(solution)/shard_map/all_to_all | solution.py:68
  (50 shorter events, 51.3 us)
Async XLA Ops:
  54.5 5.4 %copy-start.2 = (f32[2,3,128]{2,0,1:T(2,128)S(1)}, f32[2,3,128]{2,0,1:T(2,128)}, u32[]{:S(2)}) copy-start(f32[2,3,128]{2,0,1:T(2,128)} %param.5) | copy-start | bytes 9220
  54.5 53.4 %all-to-all-start.1 = ((bf16[16,512,128]{2,0,1:T(8,128)(2,1)}), bf16[16,512,128]{2,0,1:T(8,128)(2,1)}, u32[]{:S(2)}, u32[]{:S(2)}) async-start(bf16[16,512,128]{2,0,1:T(8,128)(2,1)} %copy.9), calls=%async_computation.1 | async-start | bytes 4194304 | tf_op jit(solution)/shard_map/all_to_all | solution.py:65
  110.8 1.0 copy-start.1
  117.0 9.4 %collective-permute-start.1 = (bf16[1,514,128]{2,1,0:T(8,128)(2,1)S(1)}, bf16[1,514,128]{2,1,0:T(8,128)(2,1)S(1)}, u32[]{:S(2)}, u32[]{:S(2)}) collective-permute-start(bf16[1,514,128]{2,1,0:T(8,128)(2,1)S(1)} %get-tuple-element.8), channel_id=1, source_target_pairs={{1,0},{2,1},{3,2},{4,3},{5,4},{6,5},{7,6},{8,7},{9,8},{10,9},{11,1... | collective-permute-start | bytes 394760 | tf_op jit(solution)/shard_map/ppermute | solution.py:15
  121.6 10.1 %collective-permute-start = (bf16[1,514,128]{2,1,0:T(8,128)(2,1)S(1)}, bf16[1,514,128]{2,1,0:T(8,128)(2,1)S(1)}, u32[]{:S(2)}, u32[]{:S(2)}) collective-permute-start(bf16[1,514,128]{2,1,0:T(8,128)(2,1)S(1)} %get-tuple-element.7), channel_id=1, source_target_pairs={{0,1},{1,2},{2,3},{3,4},{4,5},{5,6},{6,7},{7,8},{8,9},{9,10},{10,1... | collective-permute-start | bytes 394760 | tf_op jit(solution)/shard_map/ppermute | solution.py:14
  151.9 1.0 copy-start
  158.2 23.8 %collective-permute-start.2 = (bf16[2,516,128]{2,1,0:T(8,128)(2,1)S(1)}, bf16[2,516,128]{2,1,0:T(8,128)(2,1)S(1)}, u32[]{:S(2)}, u32[]{:S(2)}) collective-permute-start(bf16[2,516,128]{2,1,0:T(8,128)(2,1)S(1)} %get-tuple-element.15), channel_id=1, source_target_pairs={{0,1},{1,2},{2,3},{3,4},{4,5},{5,6},{6,7},{7,8},{8,9},{9,10},{10,1... | collective-permute-start | bytes 792584 | tf_op jit(solution)/shard_map/ppermute | solution.py:14
  160.6 16.0 %collective-permute-start.3 = (bf16[2,516,128]{2,1,0:T(8,128)(2,1)S(1)}, bf16[2,516,128]{2,1,0:T(8,128)(2,1)S(1)}, u32[]{:S(2)}, u32[]{:S(2)}) collective-permute-start(bf16[2,516,128]{2,1,0:T(8,128)(2,1)S(1)} %get-tuple-element.16), channel_id=1, source_target_pairs={{1,0},{2,1},{3,2},{4,3},{5,4},{6,5},{7,6},{8,7},{9,8},{10,9},{11,1... | collective-permute-start | bytes 792584 | tf_op jit(solution)/shard_map/ppermute | solution.py:15
  202.2 16.6 %collective-permute-start.5 = (bf16[4,520,128]{2,1,0:T(8,128)(2,1)S(1)}, bf16[4,520,128]{2,1,0:T(8,128)(2,1)S(1)}, u32[]{:S(2)}, u32[]{:S(2)}) collective-permute-start(bf16[4,520,128]{2,1,0:T(8,128)(2,1)S(1)} %get-tuple-element.14), channel_id=1, source_target_pairs={{1,0},{2,1},{3,2},{4,3},{5,4},{6,5},{7,6},{8,7},{9,8},{10,9},{11,1... | collective-permute-start | bytes 1597448 | tf_op jit(solution)/shard_map/ppermute | solution.py:15
  211.1 17.8 %collective-permute-start.4 = (bf16[4,520,128]{2,1,0:T(8,128)(2,1)S(1)}, bf16[4,520,128]{2,1,0:T(8,128)(2,1)S(1)}, u32[]{:S(2)}, u32[]{:S(2)}) collective-permute-start(bf16[4,520,128]{2,1,0:T(8,128)(2,1)S(1)} %get-tuple-element.13), channel_id=1, source_target_pairs={{0,1},{1,2},{2,3},{3,4},{4,5},{5,6},{6,7},{7,8},{8,9},{9,10},{10,1... | collective-permute-start | bytes 1597448 | tf_op jit(solution)/shard_map/ppermute | solution.py:14
  313.5 9.3 %collective-permute-start.7 = (bf16[1,514,128]{2,1,0:T(8,128)(2,1)S(1)}, bf16[1,514,128]{2,1,0:T(8,128)(2,1)S(1)}, u32[]{:S(2)}, u32[]{:S(2)}) collective-permute-start(bf16[1,514,128]{2,1,0:T(8,128)(2,1)S(1)} %get-tuple-element.6), channel_id=1, source_target_pairs={{1,0},{2,1},{3,2},{4,3},{5,4},{6,5},{7,6},{8,7},{9,8},{10,9},{11,1... | collective-permute-start | bytes 394760 | tf_op jit(solution)/shard_map/ppermute | solution.py:15
  318.7 9.5 %collective-permute-start.6 = (bf16[1,514,128]{2,1,0:T(8,128)(2,1)S(1)}, bf16[1,514,128]{2,1,0:T(8,128)(2,1)S(1)}, u32[]{:S(2)}, u32[]{:S(2)}) collective-permute-start(bf16[1,514,128]{2,1,0:T(8,128)(2,1)S(1)} %get-tuple-element.5), channel_id=1, source_target_pairs={{0,1},{1,2},{2,3},{3,4},{4,5},{5,6},{6,7},{7,8},{8,9},{9,10},{10,1... | collective-permute-start | bytes 394760 | tf_op jit(solution)/shard_map/ppermute | solution.py:14
  354.2 24.8 %collective-permute-start.8 = (bf16[2,516,128]{2,1,0:T(8,128)(2,1)S(1)}, bf16[2,516,128]{2,1,0:T(8,128)(2,1)S(1)}, u32[]{:S(2)}, u32[]{:S(2)}) collective-permute-start(bf16[2,516,128]{2,1,0:T(8,128)(2,1)S(1)} %get-tuple-element.11), channel_id=1, source_target_pairs={{0,1},{1,2},{2,3},{3,4},{4,5},{5,6},{6,7},{7,8},{8,9},{9,10},{10,1... | collective-permute-start | bytes 792584 | tf_op jit(solution)/shard_map/ppermute | solution.py:14
  356.8 16.9 %collective-permute-start.9 = (bf16[2,516,128]{2,1,0:T(8,128)(2,1)S(1)}, bf16[2,516,128]{2,1,0:T(8,128)(2,1)S(1)}, u32[]{:S(2)}, u32[]{:S(2)}) collective-permute-start(bf16[2,516,128]{2,1,0:T(8,128)(2,1)S(1)} %get-tuple-element.12), channel_id=1, source_target_pairs={{1,0},{2,1},{3,2},{4,3},{5,4},{6,5},{7,6},{8,7},{9,8},{10,9},{11,1... | collective-permute-start | bytes 792584 | tf_op jit(solution)/shard_map/ppermute | solution.py:15
  399.3 16.8 %collective-permute-start.11 = (bf16[4,520,128]{2,1,0:T(8,128)(2,1)S(1)}, bf16[4,520,128]{2,1,0:T(8,128)(2,1)S(1)}, u32[]{:S(2)}, u32[]{:S(2)}) collective-permute-start(bf16[4,520,128]{2,1,0:T(8,128)(2,1)S(1)} %get-tuple-element.10), channel_id=1, source_target_pairs={{1,0},{2,1},{3,2},{4,3},{5,4},{6,5},{7,6},{8,7},{9,8},{10,9},{11,1... | collective-permute-start | bytes 1597448 | tf_op jit(solution)/shard_map/ppermute | solution.py:15
  408.5 17.8 %collective-permute-start.10 = (bf16[4,520,128]{2,1,0:T(8,128)(2,1)S(1)}, bf16[4,520,128]{2,1,0:T(8,128)(2,1)S(1)}, u32[]{:S(2)}, u32[]{:S(2)}) collective-permute-start(bf16[4,520,128]{2,1,0:T(8,128)(2,1)S(1)} %get-tuple-element.9), channel_id=1, source_target_pairs={{0,1},{1,2},{2,3},{3,4},{4,5},{5,6},{6,7},{7,8},{8,9},{9,10},{10,1... | collective-permute-start | bytes 1597448 | tf_op jit(solution)/shard_map/ppermute | solution.py:14
  431.7 2.7 copy-start.3
where the time goes:
time: 508 us; the launch traced here: 501 us
  matrix products  200 us (39%)
  blocking collectives  160 us (31%)
  waiting for transfers between devices  75.9 us (15%)
  starting transfers between devices  45.1 us (9%)
  local copies, waits for them, and re-layouts  18.3 us (4%)
    dot_general x54, matrix products, convolve(): jnp.dot(piece, kernel[tap_row, tap_col], preferred_element_type=jnp.float32)  200 us
    all_to_all x1, blocking collectives, per_device(): lax.all_to_all(current, ('row', 'col'), split_axis=1, concat_axis=0, tile...  57 us
    all_to_all x1, blocking collectives, per_device(): lax.all_to_all(contact_map, 'col', split_axis=0, concat_axis=1, tiled=True)  51.7 us
    all_to_all x1, blocking collectives, per_device(): lax.all_to_all(current, 'col', split_axis=1, concat_axis=0, tiled=True)  51.5 us
    all_to_all x1, waiting for transfers between devices, per_device(): lax.all_to_all(current, ('row', 'col'), split_axis=1, concat_axis=0, tile...  45.1 us
    ppermute x6, waiting for transfers between devices, with_halo(): after = lax.ppermute(initial, axis, down)  21.2 us
    ppermute x6, starting transfers between devices, with_halo(): after = lax.ppermute(initial, axis, down)  20.5 us
    ppermute x6, starting transfers between devices, with_halo(): before = lax.ppermute(last, axis, up)  19.2 us
  transfers between devices with their start and end apart: 13, of which 7 were waited for; matrix products, arithmetic and copies ran while one was open for 13% of the time, Pallas kernels for 0%

commit v1 on v0

v1 whole, which is shorter than its diff:
```python
import functools

import jax
import jax.numpy as jnp
from jax import lax
from jax.experimental import pallas as pl
from jax.experimental.pallas import tpu as pltpu
from jax.sharding import PartitionSpec as P

BF16, F32 = jnp.bfloat16, jnp.float32
DILATIONS = (1, 2, 4)
ROW_HALO = 2 * sum(DILATIONS)
COL_HALO = 16


def pair_weights(w):
    c = w.shape[2]
    a0, a1, a2 = (w[a].reshape(3 * c, c) for a in range(3))
    zero = jnp.zeros_like(a0)
    left = jnp.concatenate([a0, a1, a2, zero], axis=0)
    right = jnp.concatenate([zero, a0, a1, a2], axis=0)
    return jnp.concatenate([left, right], axis=1)


def trunk_kernel(rows, cols, where_ref, map_ref, both_ref, wide_ref, bias_ref, out_ref,
                 buf_a, buf_b, buf_c, cur_ref, mir_ref):
    tall, wide, ch = map_ref.shape
    row0, col0, bins = where_ref[0], where_ref[1], where_ref[2]
    position = lax.broadcasted_iota(jnp.int32, (wide, ch), 0) + (col0 - COL_HALO)
    col_ok = (position >= 0) & (position < bins)

    def keep(value, row):
        place = row0 - ROW_HALO + row
        inside = (place >= 0) & (place < bins)
        return jnp.where(col_ok & inside, value, 0.0)

    def spread(dst, row, value, d):
        dst[row, :, 0:ch] = pltpu.roll(value, d, 0).astype(BF16)
        dst[row, :, ch:2 * ch] = value.astype(BF16)
        dst[row, :, 2 * ch:3 * ch] = pltpu.roll(value, wide - d, 0).astype(BF16)

    def pairs(src, weight, d, first, last, emit, cut=slice(None)):
        count = min(d, 2)
        steps = (last - first) // (2 * count)

        @pl.loop(0, steps)
        def _(step):
            if d == 4:
                r = first + (step // 2) * 8 + (step % 2) * 2
            else:
                r = first + step * 2 * count
            taps = [src[pl.ds(r + k * d, count), cut, :] for k in (-1, 0, 1, 2)]
            lhs = jnp.concatenate([t.reshape(-1, 3 * ch) for t in taps], axis=1)
            total = jnp.dot(lhs, wide_ref[weight], preferred_element_type=F32)
            n = total.shape[0] // count
            for k in range(count):
                emit(r + k, total[k * n:(k + 1) * n, :ch])
                emit(r + k + d, total[k * n:(k + 1) * n, ch:])

    def relu_into(dst, bias, d):
        def emit(row, total):
            value = jnp.maximum(total + bias_ref[bias], 0.0)
            spread(dst, row, keep(value, row), d)
        return emit

    @pl.loop(0, tall)
    def _(row):
        spread(buf_a, row, map_ref[row].astype(F32), 1)

    @pl.loop(1, tall - 1)
    def _(row):
        lhs = jnp.concatenate([buf_a[row - 1], buf_a[row], buf_a[row + 1]], axis=1)
        total = jnp.dot(lhs, both_ref[...], preferred_element_type=F32)
        relu_into(buf_b, 0, 2)(row, total[:, :ch])
        relu_into(buf_c, 0, 2)(row, total[:, ch:])

    def first_out(row, total):
        cur_ref[row] = (map_ref[row].astype(F32) + total + bias_ref[2]).astype(BF16)

    def second_out(row, total):
        other = (map_ref[row].astype(F32) + total + bias_ref[2]).astype(BF16)
        value = ((cur_ref[row].astype(F32) + other.astype(F32)) * 0.5).astype(BF16)
        value = keep(value.astype(F32), row)
        mir_ref[row] = value.astype(BF16)
        spread(buf_b, row, value, 1)

    pairs(buf_b, 0, 2, 2, tall - 2, relu_into(buf_a, 1, 4))
    pairs(buf_a, 1, 4, 6, tall - 6, first_out)
    pairs(buf_c, 2, 2, 2, tall - 2, relu_into(buf_a, 1, 4))
    pairs(buf_a, 3, 4, 6, tall - 6, second_out)

    pairs(buf_b, 4, 1, 8, tall - 8, relu_into(buf_c, 3, 2))
    pairs(buf_c, 5, 2, 10, tall - 10, relu_into(buf_a, 4, 4))

    mid = slice(COL_HALO, COL_HALO + cols)

    def last_out(row, total):
        value = mir_ref[row, mid, :].astype(F32) + total + bias_ref[5]
        out_ref[row - ROW_HALO] = value.astype(BF16)

    pairs(buf_a, 6, 4, ROW_HALO, ROW_HALO + rows, last_out, mid)


def trunk(padded, where, conv_weight, conv_bias, rows, cols):
    tall, wide, ch = padded.shape
    flip = jnp.swapaxes(conv_weight[0], 1, 2)
    both = jnp.concatenate(
        [conv_weight[0, 0].reshape(9 * ch, ch), flip[0].reshape(9 * ch, ch)], axis=1)
    wides = jnp.stack([pair_weights(w) for w in (
        conv_weight[0, 1], conv_weight[0, 2], flip[1], flip[2],
        conv_weight[1, 0], conv_weight[1, 1], conv_weight[1, 2])])
    vmem = pl.BlockSpec(memory_space=pltpu.VMEM)
    return pl.pallas_call(
        functools.partial(trunk_kernel, rows, cols),
        out_shape=jax.ShapeDtypeStruct((rows, cols, ch), BF16),
        in_specs=[pl.BlockSpec(memory_space=pltpu.SMEM)] + [vmem] * 4,
        out_specs=vmem,
        scratch_shapes=[pltpu.VMEM((tall, wide, 3 * ch), BF16)] * 3
        + [pltpu.VMEM((tall, wide, ch), BF16)] * 2,
        compiler_params=pltpu.CompilerParams(vmem_limit_bytes=60 * 1024 * 1024),
    )(where, padded, both, wides, conv_bias.reshape(6, 1, ch))


def mirror(mine):
    half = mine.shape[0]
    n_row, n_col = lax.axis_size("row"), lax.axis_size("col")
    core = lax.axis_index("row") % 2
    parts = []
    for turn in range(2):
        side = (core + turn) % 2
        piece = lax.dynamic_slice_in_dim(mine, side * half, half, axis=1)
        route = []
        for r in range(n_row):
            for c in range(n_col):
                target = (2 * c + (r + turn) % 2) * n_col + r // 2
                route.append((r * n_col + c, target))
        got = lax.ppermute(piece, ("row", "col"), route)
        parts.append(jnp.swapaxes(got, 0, 1))
    low = jnp.where(core == 0, parts[0], parts[1])
    high = jnp.where(core == 0, parts[1], parts[0])
    flipped = jnp.concatenate([low, high], axis=1)
    return ((mine.astype(F32) + flipped.astype(F32)) * 0.5).astype(BF16)


def with_halo(array, axis, dim, width):
    devices, length = lax.axis_size(axis), array.shape[dim]
    up = [(i, i + 1) for i in range(devices - 1)]
    down = [(j, i) for i, j in up]
    before = lax.ppermute(lax.slice_in_dim(array, length - width, length, axis=dim), axis, up)
    after = lax.ppermute(lax.slice_in_dim(array, 0, width, axis=dim), axis, down)
    return jnp.concatenate([before, array, after], axis=dim)


def per_device(contact_map, conv_weight, conv_bias):
    rows, cols, _ = contact_map.shape
    mirrored = mirror(contact_map)
    padded = with_halo(mirrored, "row", 0, ROW_HALO)
    padded = with_halo(padded, "col", 1, COL_HALO)
    where = jnp.stack([
        lax.axis_index("row") * rows, lax.axis_index("col") * cols, lax.axis_size("row") * rows,
    ]).astype(jnp.int32)
    return trunk(padded, where, conv_weight, conv_bias, rows, cols)


def solution(mesh):
    in_specs = (P("row", "col", None), P(), P())
    out_specs = P("row", "col", None)
    return jax.shard_map(
        per_device, mesh=mesh, in_specs=in_specs, out_specs=out_specs, check_vma=False
    )
```

time: 508 us -> 284 us (0.56); the launches traced: 501 us -> 284 us
  matrix products: 200 us -> 0 us
  blocking collectives: 160 us -> 0 us
  Pallas kernels: 0 us -> 102 us
  waiting for transfers between devices: 75.9 us -> 98.1 us
  other arithmetic: 1.56 us -> 18.3 us
  starting transfers between devices: 45.1 us -> 58.7 us
  local copies, waits for them, and re-layouts: 18.3 us -> 6.91 us
    dot_general x54 -> x0, matrix products: 200 us -> none  [convolve(): jnp.dot(piece, kernel[tap_row, tap_col], preferred_element_type=jnp.float32)]
    all_to_all x3 -> x0, blocking collectives: 160 us -> none  [the longest x1 57 us: per_device(): lax.all_to_all(current, ('row', 'col'), split_axis=1, concat_axis=0, tile...]
    pallas_call x0 -> x1, Pallas kernels: none -> 102 us  [trunk(): pl.pallas_call(functools.partial(trunk_kernel, rows, cols), out_shape=jax...]
    ppermute x12 -> x6, waiting for transfers between devices: 30.8 us -> 98.1 us  [the longest x2 83.7 us: mirror(): got = lax.ppermute(piece, ('row', 'col'), route)]
    all_to_all x1 -> x0, waiting for transfers between devices: 45.1 us -> none  [per_device(): lax.all_to_all(current, ('row', 'col'), split_axis=1, concat_axis=0, tile...]
    ppermute x12 -> x6, starting transfers between devices: 39.7 us -> 58.7 us  [the longest x2 43.3 us: with_halo(): lax.ppermute(lax.slice_in_dim(array, length - width, length, axis=dim), a...]
    concatenate x0 -> x2, other arithmetic: none -> 7.76 us  [the longest x1 6.87 us: with_halo(): return jnp.concatenate([before, array, after], axis=dim)]
    unnamed x0 -> x6, other arithmetic: none -> 5.76 us
  transfers between devices with their start and end apart: 13 -> 6, of which waited for: 7 -> 6; matrix products, arithmetic and copies ran while one was open for 13% -> 4% of each run, Pallas kernels for 0% -> 0%
where the time goes in v1:
time: 284 us
  Pallas kernels  102 us (36%)
  waiting for transfers between devices  98.1 us (35%)
  starting transfers between devices  58.7 us (21%)
  other arithmetic  18.3 us (6%)
  local copies, waits for them, and re-layouts  6.91 us (2%)
    pallas_call x1, Pallas kernels, trunk(): pl.pallas_call(functools.partial(trunk_kernel, rows, cols), out_shape=jax...  102 us
    ppermute x2, waiting for transfers between devices, mirror(): got = lax.ppermute(piece, ('row', 'col'), route)  83.7 us
    ppermute x2, starting transfers between devices, with_halo(): lax.ppermute(lax.slice_in_dim(array, length - width, length, axis=dim), a...  43.3 us
    ppermute x2, waiting for transfers between devices, with_halo(): lax.ppermute(lax.slice_in_dim(array, 0, width, axis=dim), axis, down)  12.1 us
    ppermute x2, starting transfers between devices, with_halo(): lax.ppermute(lax.slice_in_dim(array, 0, width, axis=dim), axis, down)  10.4 us
    concatenate x1, other arithmetic, with_halo(): return jnp.concatenate([before, array, after], axis=dim)  6.87 us
    unnamed x6, other arithmetic  5.76 us
  transfers between devices with their start and end apart: 6, of which 6 were waited for; matrix products, arithmetic and copies ran while one was open for 4% of the time, Pallas kernels for 0%

profile of v1, /device:TPU:12, one launch (start us, length us, event | category | flops | bytes accessed | tf_op | source)
XLA Modules:
  0.0 283.7 jit_solution(6780738074199037606)
XLA Ops:
  0.0 1.7 constant_dynamic-slice_fusion.1
  1.7 1.6 copy.13
  3.4 0.0 copy-start.1
  3.4 4.5 %collective-permute-start = (bf16[64,64,128]{2,0,1:T(8,128)(2,1)}, bf16[64,64,128]{2,0,1:T(8,128)(2,1)S(1)}, u32[]{:S(2)}, u32[]{:S(2)}) collective-permute-start(bf16[64,64,128]{2,0,1:T(8,128)(2,1)} %copy.13), channel_id=1, source_target_pairs={{0,0},{1,8},{2,16},{3,24},{4,4},{5,12},{6,20},{7,28},{8,1},{9,9},{... | collective-permute-start | bytes 3145736 | tf_op jit(solution)/shard_map/ppermute | solution.py:137
  7.9 1.7 copy.14
  9.5 0.5 collective-permute-start.1
  10.1 0.0 copy-done.1
  10.1 0.1 slice_bitcast_fusion
  10.3 0.9 pad_maximum_fusion.15.both_ref
  11.2 0.9 fusion.37
  12.0 0.1 fusion.36
  12.1 0.0 copy-start.5
  12.2 0.0 copy-start.6
  12.2 0.0 copy-start.7
  12.2 1.0 fusion.2
  13.2 1.0 fusion.5
  14.1 0.0 copy-done.5
  14.1 0.0 copy-done.6
  14.1 0.0 copy-done.7
  14.1 0.9 fusion.8
  15.1 0.0 copy-start
  15.1 63.2 %collective-permute-done = bf16[64,64,128]{2,0,1:T(8,128)(2,1)S(1)} collective-permute-done((bf16[64,64,128]{2,0,1:T(8,128)(2,1)}, bf16[64,64,128]{2,0,1:T(8,128)(2,1)S(1)}, u32[]{:S(2)}, u32[]{:S(2)}) %collective-permute-start) | collective-permute-done | bytes 1048608 | tf_op jit(solution)/shard_map/ppermute | solution.py:137
  78.3 20.5 %collective-permute-done.1 = bf16[64,64,128]{2,0,1:T(8,128)(2,1)} collective-permute-done((bf16[64,64,128]{2,0,1:T(8,128)(2,1)}, bf16[64,64,128]{2,0,1:T(8,128)(2,1)}, u32[]{:S(2)}, u32[]{:S(2)}) %collective-permute-start.1) | collective-permute-done | bytes 1048608 | tf_op jit(solution)/shard_map/ppermute | solution.py:137
  98.8 1.4 select_bitcast_fusion.1
  100.1 0.0 copy-done
  100.1 0.8 multiply_convert_fusion
  101.0 0.0 copy-start.2
  101.0 0.0 copy-start.3
  101.0 0.0 copy-start.4
  101.0 0.1 fusion.35
  101.1 2.9 %collective-permute-start.2 = (bf16[14,128,128]{2,1,0:T(8,128)(2,1)S(1)}, bf16[14,128,128]{2,1,0:T(8,128)(2,1)S(1)}, u32[]{:S(2)}, u32[]{:S(2)}) collective-permute-start(bf16[14,128,128]{2,1,0:T(8,128)(2,1)S(1)} %get-tuple-element.7), channel_id=1, source_target_pairs={{0,4},{4,8},{8,12},{12,16},{16,20},{20,24},{24,28},{1,5},{5,9},{9,... | collective-permute-start | bytes 1376264 | tf_op jit(solution)/shard_map/ppermute | solution.py:149
  104.0 3.7 %collective-permute-start.3 = (bf16[14,128,128]{2,1,0:T(8,128)(2,1)S(1)}, bf16[14,128,128]{2,1,0:T(8,128)(2,1)S(1)}, u32[]{:S(2)}, u32[]{:S(2)}) collective-permute-start(bf16[14,128,128]{2,1,0:T(8,128)(2,1)S(1)} %get-tuple-element.8), channel_id=1, source_target_pairs={{4,0},{8,4},{12,8},{16,12},{20,16},{24,20},{28,24},{5,1},{9,5},{13... | collective-permute-start | bytes 1376264 | tf_op jit(solution)/shard_map/ppermute | solution.py:150
  107.7 0.0 copy-done.2
  107.7 0.0 copy-done.3
  107.7 0.0 copy-done.4
  107.7 1.0 fusion.11
  108.7 1.0 fusion.14
  109.6 0.0 copy-start.8
  109.6 2.3 collective-permute-done.2
  111.9 2.4 collective-permute-done.3
  114.3 1.0 pad_maximum_fusion.18
  115.3 40.4 %collective-permute-start.4 = (bf16[92,16,128]{2,1,0:T(8,128)(2,1)}, bf16[92,16,128]{2,1,0:T(8,128)(2,1)}, u32[]{:S(2)}, u32[]{:S(2)}) collective-permute-start(bf16[92,16,128]{2,1,0:T(8,128)(2,1)} %get-tuple-element.5), channel_id=1, source_target_pairs={{0,1},{1,2},{2,3},{4,5},{5,6},{6,7},{8,9},{9,10},{10,11},{12,13},{... | collective-permute-start | bytes 1130504 | tf_op jit(solution)/shard_map/ppermute | solution.py:149
  155.7 6.7 %collective-permute-start.5 = (bf16[92,16,128]{2,1,0:T(8,128)(2,1)}, bf16[92,16,128]{2,1,0:T(8,128)(2,1)}, u32[]{:S(2)}, u32[]{:S(2)}) collective-permute-start(bf16[92,16,128]{2,1,0:T(8,128)(2,1)} %get-tuple-element.6), channel_id=1, source_target_pairs={{1,0},{2,1},{3,2},{5,4},{6,5},{7,6},{9,8},{10,9},{11,10},{13,12},{... | collective-permute-start | bytes 1130504 | tf_op jit(solution)/shard_map/ppermute | solution.py:150
  162.4 1.0 fusion.17
  163.3 0.0 copy-done.8
  163.3 0.6 reshape.46.bias_ref
  163.9 0.6 pad_add_fusion.where_ref
  164.6 1.0 fusion.20.wide_ref
  165.5 0.1 collective-permute-done.4
  165.6 9.7 %collective-permute-done.5 = bf16[92,16,128]{2,1,0:T(8,128)(2,1)} collective-permute-done((bf16[92,16,128]{2,1,0:T(8,128)(2,1)}, bf16[92,16,128]{2,1,0:T(8,128)(2,1)}, u32[]{:S(2)}, u32[]{:S(2)}) %collective-permute-start.5) | collective-permute-done | bytes 376864 | tf_op jit(solution)/shard_map/ppermute | solution.py:150
  175.3 6.9 %pad_maximum_fusion.map_ref = bf16[92,160,128]{2,1,0:T(8,128)(2,1)} fusion(bf16[92,16,128]{2,1,0:T(8,128)(2,1)} %collective-permute-done.5, bf16[14,128,128]{2,1,0:T(8,128)(2,1)S(1)} %collective-permute-done.3, bf16[64,128,128]{2,1,0:T(8,128)(2,1)S(1)} %multiply_convert_fusion, bf16[14,128,128]{2,1,0:T(8,128)(2,1)S(1)} %collective-permute-done.2, ...), kind=kLoop, calls=%fused_computation.1 | loop fusion | flops 18841600 | bytes 7536640 | tf_op jit(solution)/shard_map/concatenate | solution.py:151
  182.1 101.5 %shard_map.37 = bf16[64,128,128]{2,1,0:T(8,128)(2,1)} custom-call(s32[3]{0:T(128)} %pad_add_fusion.where_ref, bf16[92,160,128]{2,1,0:T(8,128)(2,1)} %pad_maximum_fusion.map_ref, bf16[1152,256]{1,0:T(8,128)(2,1)} %pad_maximum_fusion.15.both_ref, bf16[7,1536,256]{2,1,0:T(8,128)(2,1)} %fusion.20.wide_ref, f32[6,1,128]{2,1,0:T(1,128)} %reshape.46.bias_ref), custom_call_target="tpu_custom_call" | custom-call | tf_op jit(solution)/shard_map/pallas_call | solution.py:113
  (5 shorter events, 0.1 us)
Async XLA Ops:
  3.4 6.7 %copy-start.1 = (bf16[2,3,3,3,128,128]{5,4,3,2,1,0:T(8,128)(2,1)S(1)}, bf16[2,3,3,3,128,128]{5,4,3,2,1,0:T(8,128)(2,1)}, u32[]{:S(2)}) copy-start(bf16[2,3,3,3,128,128]{5,4,3,2,1,0:T(8,128)(2,1)} %param.4) | copy-start | bytes 5308420
  3.4 74.9 %collective-permute-start = (bf16[64,64,128]{2,0,1:T(8,128)(2,1)}, bf16[64,64,128]{2,0,1:T(8,128)(2,1)S(1)}, u32[]{:S(2)}, u32[]{:S(2)}) collective-permute-start(bf16[64,64,128]{2,0,1:T(8,128)(2,1)} %copy.13), channel_id=1, source_target_pairs={{0,0},{1,8},{2,16},{3,24},{4,4},{5,12},{6,20},{7,28},{8,1},{9,9},{... | collective-permute-start | bytes 3145736 | tf_op jit(solution)/shard_map/ppermute | solution.py:137
  9.5 89.2 %collective-permute-start.1 = (bf16[64,64,128]{2,0,1:T(8,128)(2,1)}, bf16[64,64,128]{2,0,1:T(8,128)(2,1)}, u32[]{:S(2)}, u32[]{:S(2)}) collective-permute-start(bf16[64,64,128]{2,0,1:T(8,128)(2,1)} %copy.14), channel_id=1, source_target_pairs={{0,4},{1,12},{2,20},{3,28},{4,0},{5,8},{6,16},{7,24},{8,5},{9,13},... | collective-permute-start | bytes 3145736 | tf_op jit(solution)/shard_map/ppermute | solution.py:137
  12.1 2.0 copy-start.5
  12.2 2.0 copy-start.6
  12.2 2.0 copy-start.7
  15.1 85.1 %copy-start = (bf16[64,128,128]{2,1,0:T(8,128)(2,1)S(1)}, bf16[64,128,128]{2,1,0:T(8,128)(2,1)}, u32[]{:S(2)}) copy-start(bf16[64,128,128]{2,1,0:T(8,128)(2,1)} %param.3) | copy-start | bytes 6291460
  101.0 6.7 %copy-start.2 = (bf16[1,1,3,128,128]{4,3,1,2,0:T(8,128)(2,1)S(1)}, bf16[1,1,3,128,128]{4,3,1,2,0:T(8,128)(2,1)}, u32[]{:S(2)}) copy-start(bf16[1,1,3,128,128]{4,3,1,2,0:T(8,128)(2,1)} %get-tuple-element.28) | copy-start | bytes 294916
  101.0 6.7 %copy-start.3 = (bf16[1,1,3,128,128]{4,3,1,2,0:T(8,128)(2,1)S(1)}, bf16[1,1,3,128,128]{4,3,1,2,0:T(8,128)(2,1)}, u32[]{:S(2)}) copy-start(bf16[1,1,3,128,128]{4,3,1,2,0:T(8,128)(2,1)} %get-tuple-element.29) | copy-start | bytes 294916
  101.0 6.7 %copy-start.4 = (bf16[1,1,3,128,128]{4,3,1,2,0:T(8,128)(2,1)S(1)}, bf16[1,1,3,128,128]{4,3,1,2,0:T(8,128)(2,1)}, u32[]{:S(2)}) copy-start(bf16[1,1,3,128,128]{4,3,1,2,0:T(8,128)(2,1)} %get-tuple-element.30) | copy-start | bytes 294916
  101.1 10.8 %collective-permute-start.2 = (bf16[14,128,128]{2,1,0:T(8,128)(2,1)S(1)}, bf16[14,128,128]{2,1,0:T(8,128)(2,1)S(1)}, u32[]{:S(2)}, u32[]{:S(2)}) collective-permute-start(bf16[14,128,128]{2,1,0:T(8,128)(2,1)S(1)} %get-tuple-element.7), channel_id=1, source_target_pairs={{0,4},{4,8},{8,12},{12,16},{16,20},{20,24},{24,28},{1,5},{5,9},{9,... | collective-permute-start | bytes 1376264 | tf_op jit(solution)/shard_map/ppermute | solution.py:149
  104.0 10.3 %collective-permute-start.3 = (bf16[14,128,128]{2,1,0:T(8,128)(2,1)S(1)}, bf16[14,128,128]{2,1,0:T(8,128)(2,1)S(1)}, u32[]{:S(2)}, u32[]{:S(2)}) collective-permute-start(bf16[14,128,128]{2,1,0:T(8,128)(2,1)S(1)} %get-tuple-element.8), channel_id=1, source_target_pairs={{4,0},{8,4},{12,8},{16,12},{20,16},{24,20},{28,24},{5,1},{9,5},{13... | collective-permute-start | bytes 1376264 | tf_op jit(solution)/shard_map/ppermute | solution.py:150
  109.6 53.7 %copy-start.8 = (f32[2,3,128]{2,0,1:T(2,128)S(1)}, f32[2,3,128]{2,0,1:T(2,128)}, u32[]{:S(2)}) copy-start(f32[2,3,128]{2,0,1:T(2,128)} %param.5) | copy-start | bytes 9220
  115.3 50.3 %collective-permute-start.4 = (bf16[92,16,128]{2,1,0:T(8,128)(2,1)}, bf16[92,16,128]{2,1,0:T(8,128)(2,1)}, u32[]{:S(2)}, u32[]{:S(2)}) collective-permute-start(bf16[92,16,128]{2,1,0:T(8,128)(2,1)} %get-tuple-element.5), channel_id=1, source_target_pairs={{0,1},{1,2},{2,3},{4,5},{5,6},{6,7},{8,9},{9,10},{10,11},{12,13},{... | collective-permute-start | bytes 1130504 | tf_op jit(solution)/shard_map/ppermute | solution.py:149
  155.7 19.6 %collective-permute-start.5 = (bf16[92,16,128]{2,1,0:T(8,128)(2,1)}, bf16[92,16,128]{2,1,0:T(8,128)(2,1)}, u32[]{:S(2)}, u32[]{:S(2)}) collective-permute-start(bf16[92,16,128]{2,1,0:T(8,128)(2,1)} %get-tuple-element.6), channel_id=1, source_target_pairs={{1,0},{2,1},{3,2},{5,4},{6,5},{7,6},{9,8},{10,9},{11,10},{13,12},{... | collective-permute-start | bytes 1130504 | tf_op jit(solution)/shard_map/ppermute | solution.py:150

commit v2 on v1

--- a/solution.py
+++ b/solution.py
@@ -11,6 +11,8 @@
 DILATIONS = (1, 2, 4)
 ROW_HALO = 2 * sum(DILATIONS)
 COL_HALO = 16
+CHUNKS = 8
+MESH = pl.DeviceIdType.MESH
 
 
 def pair_weights(w):
@@ -121,24 +123,171 @@
     )(where, padded, both, wides, conv_bias.reshape(6, 1, ch))
 
 
+def exchange_kernel(via_source, n_col, map_ref, out_ref, stage_ref,
+                    send_sem, recv_sem, stage_sem, pass_sem, own_sem):
+    row, col = lax.axis_index("row"), lax.axis_index("col")
+    a, e, b = row // 2, row % 2, col
+    half = map_ref.shape[0]
+    size = half // CHUNKS
+    diagonal = a == b
+
+    def relayed(source, target, k):
+        inner_source = (source > 0) & (source < n_col - 1)
+        inner_target = (target > 0) & (target < n_col - 1)
+        gap = source - target
+        near = ((gap == 1) | (gap == -1)) & (inner_source != inner_target)
+        inner = inner_source if via_source else inner_target
+        most, some, few = k % 4 != 0, k % 2 == 1, k % 4 == 3
+        share = jnp.where(near, jnp.where(inner, most, few), some)
+        return (source != target) & share
+
+    def piece(k, f):
+        return map_ref.at[pl.ds(k * size, size), pl.ds(f * half, half), :]
+
+    def land(core, k):
+        return out_ref.at[core, pl.ds(k * size, size)]
+
+    def signal(r, c):
+        pl.semaphore_signal(barrier, inc=1, device_id=(r, c), device_id_type=MESH)
+
+    barrier = pltpu.get_barrier_semaphore()
+
+    @pl.when(jnp.logical_not(diagonal))
+    def _():
+        for f in range(2):
+            signal(2 * b + f, a)
+            signal(2 * b + f, b)
+        signal(2 * a + e, a)
+        pl.semaphore_wait(barrier, 5)
+
+    @pl.when(diagonal)
+    def _():
+        signal(2 * a + 1 - e, a)
+        for s in range(1, n_col):
+            other = lax.rem(a + s, n_col)
+            if via_source:
+                signal(2 * a + e, other)
+                signal(2 * other, a)
+                signal(2 * other + 1, a)
+            else:
+                signal(2 * other, a)
+                signal(2 * other + 1, a)
+                signal(2 * a + e, other)
+        pl.semaphore_wait(barrier, 3 * (n_col - 1) + 1)
+
+    def direct(k, f):
+        return pltpu.make_async_remote_copy(
+            src_ref=piece(k, f), dst_ref=land(e, k), send_sem=send_sem.at[f, k],
+            recv_sem=recv_sem.at[e, k], device_id=(2 * b + f, a), device_id_type=MESH)
+
+    def first_hop(k, f):
+        if via_source:
+            slot, place = (b, f, k), (2 * a + e, a)
+        else:
+            slot, place = (a, e, k), (2 * b + f, b)
+        return pltpu.make_async_remote_copy(
+            src_ref=piece(k, f), dst_ref=stage_ref.at[slot], send_sem=send_sem.at[f, k],
+            recv_sem=stage_sem.at[slot], device_id=place, device_id_type=MESH)
+
+    def second_hop(k, other, bit):
+        if via_source:
+            core, place = e, (2 * other + bit, a)
+        else:
+            core, place = bit, (2 * a + e, other)
+        return pltpu.make_async_remote_copy(
+            src_ref=stage_ref.at[other, bit, k], dst_ref=land(core, k),
+            send_sem=pass_sem.at[other, bit, k], recv_sem=recv_sem.at[core, k],
+            device_id=place, device_id_type=MESH)
+
+    def own(k):
+        return pltpu.make_async_copy(piece(k, e), land(e, k), own_sem.at[k])
+
+    order = [k for k in range(CHUNKS) if k % 2] + [k for k in range(CHUNKS) if k % 2 == 0]
+
+    @pl.when(jnp.logical_not(diagonal))
+    def _():
+        for k in order:
+            for f in range(2):
+                through = relayed(a, b, k)
+
+                @pl.when(through)
+                def _():
+                    first_hop(k, f).start()
+
+                @pl.when(jnp.logical_not(through))
+                def _():
+                    direct(k, f).start()
+
+        for k in range(CHUNKS):
+            for f in range(2):
+                direct(k, f).wait_send()
+                pltpu.make_async_remote_copy(
+                    src_ref=land(f, k), dst_ref=land(f, k), send_sem=send_sem.at[f, k],
+                    recv_sem=recv_sem.at[f, k], device_id=(2 * b + f, a),
+                    device_id_type=MESH).wait_recv()
+
+    def cross(k):
+        return pltpu.make_async_remote_copy(
+            src_ref=piece(k, 1 - e), dst_ref=land(e, k), send_sem=send_sem.at[0, k],
+            recv_sem=recv_sem.at[e, k], device_id=(2 * a + 1 - e, a), device_id_type=MESH)
+
+    def crossed(k):
+        return pltpu.make_async_remote_copy(
+            src_ref=land(1 - e, k), dst_ref=land(1 - e, k), send_sem=send_sem.at[0, k],
+            recv_sem=recv_sem.at[1 - e, k], device_id=(2 * a + 1 - e, a), device_id_type=MESH)
+
+    @pl.when(diagonal)
+    def _():
+        for k in range(CHUNKS):
+            cross(k).start()
+            own(k).start()
+
+        def hops(act):
+            for k in order:
+                for s in range(1, n_col):
+                    other = lax.rem(a + s, n_col)
+                    source, target = (a, other) if via_source else (other, a)
+                    for bit in range(2):
+                        @pl.when(relayed(source, target, k))
+                        def _():
+                            act(second_hop(k, other, bit), k, other, bit)
+
+        def forward(copy, k, other, bit):
+            pltpu.make_async_remote_copy(
+                src_ref=stage_ref.at[other, bit, k], dst_ref=stage_ref.at[other, bit, k],
+                send_sem=pass_sem.at[other, bit, k], recv_sem=stage_sem.at[other, bit, k],
+                device_id=(2 * a + 1 - e, a), device_id_type=MESH).wait_recv()
+            copy.start()
+
+        hops(forward)
+        hops(lambda copy, k, other, bit: copy.wait_send())
+        for k in range(CHUNKS):
+            cross(k).wait_send()
+            crossed(k).wait_recv()
+            own(k).wait()
+
+
+def exchange(mine, via_source=False):
+    half, _, ch = mine.shape
+    n_col = lax.axis_size("col")
+    anywhere = pl.BlockSpec(memory_space=pl.ANY)
+    out, _ = pl.pallas_call(
+        functools.partial(exchange_kernel, via_source, n_col),
+        out_shape=(jax.ShapeDtypeStruct((2, half, half, ch), BF16),
+                   jax.ShapeDtypeStruct((n_col, 2, CHUNKS, half // CHUNKS, half, ch), BF16)),
+        in_specs=[anywhere], out_specs=(anywhere, anywhere),
+        scratch_shapes=[
+            pltpu.SemaphoreType.DMA((2, CHUNKS)), pltpu.SemaphoreType.DMA((2, CHUNKS)),
+            pltpu.SemaphoreType.DMA((n_col, 2, CHUNKS)), pltpu.SemaphoreType.DMA((n_col, 2, CHUNKS)),
+            pltpu.SemaphoreType.DMA((CHUNKS,))],
+        compiler_params=pltpu.CompilerParams(collective_id=0, has_side_effects=True),
+    )(mine)
+    return out
+
+
 def mirror(mine):
-    half = mine.shape[0]
-    n_row, n_col = lax.axis_size("row"), lax.axis_size("col")
-    core = lax.axis_index("row") % 2
-    parts = []
-    for turn in range(2):
-        side = (core + turn) % 2
-        piece = lax.dynamic_slice_in_dim(mine, side * half, half, axis=1)
-        route = []
-        for r in range(n_row):
-            for c in range(n_col):
-                target = (2 * c + (r + turn) % 2) * n_col + r // 2
-                route.append((r * n_col + c, target))
-        got = lax.ppermute(piece, ("row", "col"), route)
-        parts.append(jnp.swapaxes(got, 0, 1))
-    low = jnp.where(core == 0, parts[0], parts[1])
-    high = jnp.where(core == 0, parts[1], parts[0])
-    flipped = jnp.concatenate([low, high], axis=1)
+    half, full, ch = mine.shape
+    flipped = jnp.swapaxes(exchange(mine).reshape(full, half, ch), 0, 1)
     return ((mine.astype(F32) + flipped.astype(F32)) * 0.5).astype(BF16)
 
 

time: 284 us -> 231 us (0.81)
  the two profiles are of different devices: /device:TPU:12 before, /device:TPU:17 now
where the time goes in v2:
time: 231 us
  Pallas kernels  189 us (82%)
  other arithmetic  16.7 us (7%)
  starting transfers between devices  12.8 us (6%)
  waiting for transfers between devices  7.76 us (3%)
  local copies, waits for them, and re-layouts  4.05 us (2%)
    pallas_call x1, Pallas kernels, trunk(): pl.pallas_call(functools.partial(trunk_kernel, rows, cols), out_shape=jax...  102 us
    pallas_call x1, Pallas kernels, exchange(): pl.pallas_call(functools.partial(exchange_kernel, via_source, n_col), out...  87.7 us
    ppermute x2, starting transfers between devices, with_halo(): lax.ppermute(lax.slice_in_dim(array, length - width, length, axis=dim), a...  8.45 us
    concatenate x1, other arithmetic, with_halo(): return jnp.concatenate([before, array, after], axis=dim)  6.85 us
    unnamed x6, other arithmetic  5.72 us
    ppermute x2, waiting for transfers between devices, with_halo(): lax.ppermute(lax.slice_in_dim(array, 0, width, axis=dim), axis, down)  5.38 us
  transfers between devices with their start and end apart: 4, of which 3 were waited for; matrix products, arithmetic and copies ran while one was open for 4% of the time, Pallas kernels for 0%

profile of v2, /device:TPU:17, one launch (start us, length us, event | category | flops | bytes accessed | tf_op | source)
XLA Modules:
  0.0 230.7 jit_solution(8608719078511144358)
XLA Ops:
  0.0 87.7 %shard_map.37 = (bf16[2,64,64,128]{3,2,1,0:T(8,128)(2,1)}, bf16[4,2,8,8,64,128]{5,4,3,2,1,0:T(8,128)(2,1)}) custom-call(bf16[64,128,128]{2,1,0:T(8,128)(2,1)} %map_ref.1), custom_call_target="tpu_custom_call" | custom-call | tf_op jit(solution)/shard_map/pallas_call | solution.py:274
  87.7 0.0 copy-start
  87.7 3.0 %copy.7 = f32[2,64,64,128]{3,1,0,2:T(8,128)S(1)} copy(bf16[2,64,64,128]{3,2,1,0:T(8,128)(2,1)} %get-tuple-element.6) | data formatting | bytes 6291456 | tf_op jit(solution)/shard_map/convert_element_type | solution.py:291
  90.7 0.0 copy-done
  90.7 0.7 fusion.1
  91.4 0.0 copy-start.1
  91.4 0.1 fusion.37
  91.5 2.1 collective-permute-start
  93.6 2.4 %collective-permute-start.1 = (bf16[14,128,128]{2,1,0:T(8,128)(2,1)S(1)}, bf16[14,128,128]{2,1,0:T(8,128)(2,1)S(1)}, u32[]{:S(2)}, u32[]{:S(2)}) collective-permute-start(bf16[14,128,128]{2,1,0:T(8,128)(2,1)S(1)} %get-tuple-element.10), channel_id=1, source_target_pairs={{4,0},{8,4},{12,8},{16,12},{20,16},{24,20},{28,24},{5,1},{9,5},{13... | collective-permute-start | bytes 1376264 | tf_op jit(solution)/shard_map/ppermute | solution.py:299
  96.0 0.0 copy-done.1
  96.1 0.1 slice_bitcast_fusion
  96.2 0.2 fusion.38
  96.4 0.9 pad_maximum_fusion.15.both_ref
  97.3 1.0 fusion.4
  98.3 1.0 fusion.7
  99.3 0.9 fusion.10
  100.2 0.9 fusion.13
  101.1 1.0 fusion.16
  102.1 0.0 copy-start.2
  102.1 0.0 collective-permute-done
  102.1 1.3 collective-permute-done.1
  103.4 1.0 pad_maximum_fusion.18
  104.4 6.4 %collective-permute-start.2 = (bf16[92,16,128]{2,1,0:T(8,128)(2,1)}, bf16[92,16,128]{2,1,0:T(8,128)(2,1)}, u32[]{:S(2)}, u32[]{:S(2)}) collective-permute-start(bf16[92,16,128]{2,1,0:T(8,128)(2,1)} %get-tuple-element.7), channel_id=1, source_target_pairs={{0,1},{1,2},{2,3},{4,5},{5,6},{6,7},{8,9},{9,10},{10,11},{12,13},{... | collective-permute-start | bytes 1130504 | tf_op jit(solution)/shard_map/ppermute | solution.py:298
  110.8 1.9 collective-permute-start.3
  112.7 0.9 fusion.19
  113.7 0.0 copy-done.2
  113.7 0.6 reshape.50.bias_ref
  114.3 0.6 pad_add_fusion.where_ref
  114.9 1.0 fusion.22.wide_ref
  115.9 2.4 %collective-permute-done.2 = bf16[92,16,128]{2,1,0:T(8,128)(2,1)} collective-permute-done((bf16[92,16,128]{2,1,0:T(8,128)(2,1)}, bf16[92,16,128]{2,1,0:T(8,128)(2,1)}, u32[]{:S(2)}, u32[]{:S(2)}) %collective-permute-start.2) | collective-permute-done | bytes 376864 | tf_op jit(solution)/shard_map/ppermute | solution.py:298
  118.2 4.1 %collective-permute-done.3 = bf16[92,16,128]{2,1,0:T(8,128)(2,1)} collective-permute-done((bf16[92,16,128]{2,1,0:T(8,128)(2,1)}, bf16[92,16,128]{2,1,0:T(8,128)(2,1)}, u32[]{:S(2)}, u32[]{:S(2)}) %collective-permute-start.3) | collective-permute-done | bytes 376864 | tf_op jit(solution)/shard_map/ppermute | solution.py:299
  122.3 6.8 %pad_maximum_fusion.map_ref = bf16[92,160,128]{2,1,0:T(8,128)(2,1)} fusion(bf16[92,16,128]{2,1,0:T(8,128)(2,1)} %collective-permute-done.3, bf16[14,128,128]{2,1,0:T(8,128)(2,1)S(1)} %collective-permute-done.1, bf16[64,128,128]{2,1,0:T(8,128)(2,1)S(1)} %fusion.1, bf16[14,128,128]{2,1,0:T(8,128)(2,1)S(1)} %collective-permute-done, ...), kind=kLoop, calls=%fused_computation.3 | loop fusion | flops 18841600 | bytes 7536640 | tf_op jit(solution)/shard_map/concatenate | solution.py:300
  129.2 101.5 %shard_map.38 = bf16[64,128,128]{2,1,0:T(8,128)(2,1)} custom-call(s32[3]{0:T(128)} %pad_add_fusion.where_ref, bf16[92,160,128]{2,1,0:T(8,128)(2,1)} %pad_maximum_fusion.map_ref, bf16[1152,256]{1,0:T(8,128)(2,1)} %pad_maximum_fusion.15.both_ref, bf16[7,1536,256]{2,1,0:T(8,128)(2,1)} %fusion.22.wide_ref, f32[6,1,128]{2,1,0:T(1,128)} %reshape.50.bias_ref), custom_call_target="tpu_custom_call" | custom-call | tf_op jit(solution)/shard_map/pallas_call | solution.py:115
  (6 shorter events, 0.1 us)
Async XLA Ops:
  87.7 3.0 %copy-start = (bf16[64,128,128]{2,1,0:T(8,128)(2,1)S(1)}, bf16[64,128,128]{2,1,0:T(8,128)(2,1)}, u32[]{:S(2)}) copy-start(bf16[64,128,128]{2,1,0:T(8,128)(2,1)} %map_ref.1) | copy-start | bytes 6291460
  91.4 4.6 %copy-start.1 = (bf16[2,3,3,3,128,128]{5,4,3,2,1,0:T(8,128)(2,1)S(1)}, bf16[2,3,3,3,128,128]{5,4,3,2,1,0:T(8,128)(2,1)}, u32[]{:S(2)}) copy-start(bf16[2,3,3,3,128,128]{5,4,3,2,1,0:T(8,128)(2,1)} %param.4) | copy-start | bytes 5308420
  91.5 10.6 %collective-permute-start = (bf16[14,128,128]{2,1,0:T(8,128)(2,1)S(1)}, bf16[14,128,128]{2,1,0:T(8,128)(2,1)S(1)}, u32[]{:S(2)}, u32[]{:S(2)}) collective-permute-start(bf16[14,128,128]{2,1,0:T(8,128)(2,1)S(1)} %get-tuple-element.9), channel_id=1, source_target_pairs={{0,4},{4,8},{8,12},{12,16},{16,20},{20,24},{24,28},{1,5},{5,9},{9,... | collective-permute-start | bytes 1376264 | tf_op jit(solution)/shard_map/ppermute | solution.py:298
  93.6 9.8 %collective-permute-start.1 = (bf16[14,128,128]{2,1,0:T(8,128)(2,1)S(1)}, bf16[14,128,128]{2,1,0:T(8,128)(2,1)S(1)}, u32[]{:S(2)}, u32[]{:S(2)}) collective-permute-start(bf16[14,128,128]{2,1,0:T(8,128)(2,1)S(1)} %get-tuple-element.10), channel_id=1, source_target_pairs={{4,0},{8,4},{12,8},{16,12},{20,16},{24,20},{28,24},{5,1},{9,5},{13... | collective-permute-start | bytes 1376264 | tf_op jit(solution)/shard_map/ppermute | solution.py:299
  102.1 11.6 %copy-start.2 = (f32[2,3,128]{2,0,1:T(2,128)S(1)}, f32[2,3,128]{2,0,1:T(2,128)}, u32[]{:S(2)}) copy-start(f32[2,3,128]{2,0,1:T(2,128)} %param.5) | copy-start | bytes 9220
  104.4 13.9 %collective-permute-start.2 = (bf16[92,16,128]{2,1,0:T(8,128)(2,1)}, bf16[92,16,128]{2,1,0:T(8,128)(2,1)}, u32[]{:S(2)}, u32[]{:S(2)}) collective-permute-start(bf16[92,16,128]{2,1,0:T(8,128)(2,1)} %get-tuple-element.7), channel_id=1, source_target_pairs={{0,1},{1,2},{2,3},{4,5},{5,6},{6,7},{8,9},{9,10},{10,11},{12,13},{... | collective-permute-start | bytes 1130504 | tf_op jit(solution)/shard_map/ppermute | solution.py:298
  110.8 11.6 %collective-permute-start.3 = (bf16[92,16,128]{2,1,0:T(8,128)(2,1)}, bf16[92,16,128]{2,1,0:T(8,128)(2,1)}, u32[]{:S(2)}, u32[]{:S(2)}) collective-permute-start(bf16[92,16,128]{2,1,0:T(8,128)(2,1)} %get-tuple-element.8), channel_id=1, source_target_pairs={{1,0},{2,1},{3,2},{5,4},{6,5},{7,6},{9,8},{10,9},{11,10},{13,12},{... | collective-permute-start | bytes 1130504 | tf_op jit(solution)/shard_map/ppermute | solution.py:299

commit v3 on v2

--- a/solution.py
+++ b/solution.py
@@ -11,21 +11,14 @@
 DILATIONS = (1, 2, 4)
 ROW_HALO = 2 * sum(DILATIONS)
 COL_HALO = 16
+FIRST, PAIRS = 5, 4
+WIDE = ((1, False), (2, False), (1, True), (2, True), (3, False), (4, False), (5, False))
 CHUNKS = 8
 MESH = pl.DeviceIdType.MESH
 
 
-def pair_weights(w):
-    c = w.shape[2]
-    a0, a1, a2 = (w[a].reshape(3 * c, c) for a in range(3))
-    zero = jnp.zeros_like(a0)
-    left = jnp.concatenate([a0, a1, a2, zero], axis=0)
-    right = jnp.concatenate([zero, a0, a1, a2], axis=0)
-    return jnp.concatenate([left, right], axis=1)
-
-
-def trunk_kernel(rows, cols, where_ref, map_ref, both_ref, wide_ref, bias_ref, out_ref,
-                 buf_a, buf_b, buf_c, cur_ref, mir_ref):
+def trunk_kernel(rows, cols, where_ref, left_ref, mid_ref, right_ref, weight_ref, bias_ref, out_ref,
+                 buf_a, buf_b, buf_c, cur_ref, mir_ref, map_ref, both_ref, wide_ref):
     tall, wide, ch = map_ref.shape
     row0, col0, bins = where_ref[0], where_ref[1], where_ref[2]
     position = lax.broadcasted_iota(jnp.int32, (wide, ch), 0) + (col0 - COL_HALO)
@@ -41,23 +34,19 @@
         dst[row, :, ch:2 * ch] = value.astype(BF16)
         dst[row, :, 2 * ch:3 * ch] = pltpu.roll(value, wide - d, 0).astype(BF16)
 
-    def pairs(src, weight, d, first, last, emit, cut=slice(None)):
-        count = min(d, 2)
-        steps = (last - first) // (2 * count)
-
-        @pl.loop(0, steps)
+    def pairs(src, weight, d, first, last, emit, count, cut=slice(None)):
+        @pl.loop(0, (last - first) // (2 * count))
         def _(step):
-            if d == 4:
-                r = first + (step // 2) * 8 + (step % 2) * 2
-            else:
-                r = first + step * 2 * count
-            taps = [src[pl.ds(r + k * d, count), cut, :] for k in (-1, 0, 1, 2)]
-            lhs = jnp.concatenate([t.reshape(-1, 3 * ch) for t in taps], axis=1)
+            base = first + step * (2 * count)
+            tops = [base + (i // d) * 2 * d + i % d for i in range(count)]
+            lhs = jnp.concatenate([
+                jnp.concatenate([src[r + k * d, cut, :] for k in (-1, 0, 1, 2)], axis=1)
+                for r in tops], axis=0)
             total = jnp.dot(lhs, wide_ref[weight], preferred_element_type=F32)
             n = total.shape[0] // count
-            for k in range(count):
-                emit(r + k, total[k * n:(k + 1) * n, :ch])
-                emit(r + k + d, total[k * n:(k + 1) * n, ch:])
+            for i, r in enumerate(tops):
+                emit(r, total[i * n:(i + 1) * n, :ch])
+                emit(r + d, total[i * n:(i + 1) * n, ch:])
 
     def relu_into(dst, bias, d):
         def emit(row, total):
@@ -65,16 +54,34 @@
             spread(dst, row, keep(value, row), d)
         return emit
 
+    for slot, (layer, flip) in enumerate(WIDE):
+        zero = jnp.zeros((3 * ch, ch), BF16)
+        wide_ref[slot, 9 * ch:12 * ch, 0:ch] = zero
+        wide_ref[slot, 0:3 * ch, ch:2 * ch] = zero
+        for tap in range(9):
+            block = weight_ref[layer * 9 + (tap % 3 * 3 + tap // 3 if flip else tap)]
+            wide_ref[slot, tap * ch:(tap + 1) * ch, 0:ch] = block
+            wide_ref[slot, (tap + 3) * ch:(tap + 4) * ch, ch:2 * ch] = block
+    for tap in range(9):
+        both_ref[tap * ch:(tap + 1) * ch, 0:ch] = weight_ref[tap]
+        both_ref[tap * ch:(tap + 1) * ch, ch:2 * ch] = weight_ref[tap % 3 * 3 + tap // 3]
+
     @pl.loop(0, tall)
     def _(row):
+        map_ref[row, 0:COL_HALO] = left_ref[row]
+        map_ref[row, COL_HALO:COL_HALO + cols] = mid_ref[row]
+        map_ref[row, COL_HALO + cols:wide] = right_ref[row]
         spread(buf_a, row, map_ref[row].astype(F32), 1)
 
-    @pl.loop(1, tall - 1)
-    def _(row):
-        lhs = jnp.concatenate([buf_a[row - 1], buf_a[row], buf_a[row + 1]], axis=1)
+    @pl.loop(0, (tall - 2) // FIRST)
+    def _(step):
+        rows_here = [1 + step * FIRST + i for i in range(FIRST)]
+        lhs = jnp.concatenate([
+            jnp.concatenate([buf_a[row + k] for k in (-1, 0, 1)], axis=1) for row in rows_here], axis=0)
         total = jnp.dot(lhs, both_ref[...], preferred_element_type=F32)
-        relu_into(buf_b, 0, 2)(row, total[:, :ch])
-        relu_into(buf_c, 0, 2)(row, total[:, ch:])
+        for i, row in enumerate(rows_here):
+            relu_into(buf_b, 0, 2)(row, total[i * wide:(i + 1) * wide, :ch])
+            relu_into(buf_c, 0, 2)(row, total[i * wide:(i + 1) * wide, ch:])
 
     def first_out(row, total):
         cur_ref[row] = (map_ref[row].astype(F32) + total + bias_ref[2]).astype(BF16)
@@ -86,13 +93,13 @@
         mir_ref[row] = value.astype(BF16)
         spread(buf_b, row, value, 1)
 
-    pairs(buf_b, 0, 2, 2, tall - 2, relu_into(buf_a, 1, 4))
-    pairs(buf_a, 1, 4, 6, tall - 6, first_out)
-    pairs(buf_c, 2, 2, 2, tall - 2, relu_into(buf_a, 1, 4))
-    pairs(buf_a, 3, 4, 6, tall - 6, second_out)
-
-    pairs(buf_b, 4, 1, 8, tall - 8, relu_into(buf_c, 3, 2))
-    pairs(buf_c, 5, 2, 10, tall - 10, relu_into(buf_a, 4, 4))
+    pairs(buf_b, 0, 2, 2, tall - 2, relu_into(buf_a, 1, 4), PAIRS)
+    pairs(buf_a, 1, 4, 6, tall - 6, first_out, PAIRS)
+    pairs(buf_c, 2, 2, 2, tall - 2, relu_into(buf_a, 1, 4), PAIRS)
+    pairs(buf_a, 3, 4, 6, tall - 6, second_out, PAIRS)
+
+    pairs(buf_b, 4, 1, 8, tall - 8, relu_into(buf_c, 3, 2), 2)
+    pairs(buf_c, 5, 2, 10, tall - 10, relu_into(buf_a, 4, 4), PAIRS)
 
     mid = slice(COL_HALO, COL_HALO + cols)
 
@@ -100,27 +107,23 @@
         value = mir_ref[row, mid, :].astype(F32) + total + bias_ref[5]
         out_ref[row - ROW_HALO] = value.astype(BF16)
 
-    pairs(buf_a, 6, 4, ROW_HALO, ROW_HALO + rows, last_out, mid)
-
-
-def trunk(padded, where, conv_weight, conv_bias, rows, cols):
-    tall, wide, ch = padded.shape
-    flip = jnp.swapaxes(conv_weight[0], 1, 2)
-    both = jnp.concatenate(
-        [conv_weight[0, 0].reshape(9 * ch, ch), flip[0].reshape(9 * ch, ch)], axis=1)
-    wides = jnp.stack([pair_weights(w) for w in (
-        conv_weight[0, 1], conv_weight[0, 2], flip[1], flip[2],
-        conv_weight[1, 0], conv_weight[1, 1], conv_weight[1, 2])])
+    pairs(buf_a, 6, 4, ROW_HALO, ROW_HALO + rows, last_out, PAIRS, mid)
+
+
+def trunk(pieces, where, conv_weight, conv_bias, rows, cols):
+    tall, _, ch = pieces[1].shape
+    wide = cols + 2 * COL_HALO
     vmem = pl.BlockSpec(memory_space=pltpu.VMEM)
     return pl.pallas_call(
         functools.partial(trunk_kernel, rows, cols),
         out_shape=jax.ShapeDtypeStruct((rows, cols, ch), BF16),
-        in_specs=[pl.BlockSpec(memory_space=pltpu.SMEM)] + [vmem] * 4,
+        in_specs=[pl.BlockSpec(memory_space=pltpu.SMEM)] + [vmem] * 5,
         out_specs=vmem,
         scratch_shapes=[pltpu.VMEM((tall, wide, 3 * ch), BF16)] * 3
-        + [pltpu.VMEM((tall, wide, ch), BF16)] * 2,
-        compiler_params=pltpu.CompilerParams(vmem_limit_bytes=60 * 1024 * 1024),
-    )(where, padded, both, wides, conv_bias.reshape(6, 1, ch))
+        + [pltpu.VMEM((tall, wide, ch), BF16)] * 3
+        + [pltpu.VMEM((9 * ch, 2 * ch), BF16), pltpu.VMEM((len(WIDE), 12 * ch, 2 * ch), BF16)],
+        compiler_params=pltpu.CompilerParams(vmem_limit_bytes=62 * 1024 * 1024),
+    )(where, *pieces, conv_weight.reshape(54, ch, ch), conv_bias.reshape(6, 1, ch))
 
 
 def exchange_kernel(via_source, n_col, map_ref, out_ref, stage_ref,
@@ -137,8 +140,7 @@
         gap = source - target
         near = ((gap == 1) | (gap == -1)) & (inner_source != inner_target)
         inner = inner_source if via_source else inner_target
-        most, some, few = k % 4 != 0, k % 2 == 1, k % 4 == 3
-        share = jnp.where(near, jnp.where(inner, most, few), some)
+        share = jnp.where(near, inner, k % 2 == 1)
         return (source != target) & share
 
     def piece(k, f):
@@ -202,7 +204,7 @@
     def own(k):
         return pltpu.make_async_copy(piece(k, e), land(e, k), own_sem.at[k])
 
-    order = [k for k in range(CHUNKS) if k % 2] + [k for k in range(CHUNKS) if k % 2 == 0]
+    order = list(range(CHUNKS))
 
     @pl.when(jnp.logical_not(diagonal))
     def _():
@@ -291,24 +293,24 @@
     return ((mine.astype(F32) + flipped.astype(F32)) * 0.5).astype(BF16)
 
 
-def with_halo(array, axis, dim, width):
+def halo(array, axis, dim, width):
     devices, length = lax.axis_size(axis), array.shape[dim]
     up = [(i, i + 1) for i in range(devices - 1)]
     down = [(j, i) for i, j in up]
     before = lax.ppermute(lax.slice_in_dim(array, length - width, length, axis=dim), axis, up)
     after = lax.ppermute(lax.slice_in_dim(array, 0, width, axis=dim), axis, down)
-    return jnp.concatenate([before, array, after], axis=dim)
+    return before, array, after
 
 
 def per_device(contact_map, conv_weight, conv_bias):
     rows, cols, _ = contact_map.shape
     mirrored = mirror(contact_map)
-    padded = with_halo(mirrored, "row", 0, ROW_HALO)
-    padded = with_halo(padded, "col", 1, COL_HALO)
+    tall = jnp.concatenate(halo(mirrored, "row", 0, ROW_HALO), axis=0)
+    pieces = halo(tall, "col", 1, COL_HALO)
     where = jnp.stack([
         lax.axis_index("row") * rows, lax.axis_index("col") * cols, lax.axis_size("row") * rows,
     ]).astype(jnp.int32)
-    return trunk(padded, where, conv_weight, conv_bias, rows, cols)
+    return trunk(pieces, where, conv_weight, conv_bias, rows, cols)
 
 
 def solution(mesh):

time: 231 us -> 189 us (0.82)
  the two profiles are of different devices: /device:TPU:17 before, /device:TPU:12 now
where the time goes in v3:
time: 189 us; the launch traced here: 187 us
  Pallas kernels  152 us (80%)
  waiting for transfers between devices  14.7 us (8%)
  starting transfers between devices  12.3 us (7%)
  local copies, waits for them, and re-layouts  6.1 us (3%)
    pallas_call x1, Pallas kernels, exchange(): pl.pallas_call(functools.partial(exchange_kernel, via_source, n_col), out...  76.7 us
    pallas_call x1, Pallas kernels, trunk(): pl.pallas_call(functools.partial(trunk_kernel, rows, cols), out_shape=jax...  75.3 us
    ppermute x2, waiting for transfers between devices, halo(): lax.ppermute(lax.slice_in_dim(array, length - width, length, axis=dim), a...  11.6 us
    ppermute x2, starting transfers between devices, halo(): lax.ppermute(lax.slice_in_dim(array, 0, width, axis=dim), axis, down)  6.37 us
    ppermute x2, starting transfers between devices, halo(): lax.ppermute(lax.slice_in_dim(array, length - width, length, axis=dim), a...  5.95 us
  transfers between devices with their start and end apart: 4, of which 4 were waited for; matrix products, arithmetic and copies ran while one was open for 1% of the time, Pallas kernels for 0%

profile of v3, /device:TPU:12, one launch (start us, length us, event | category | flops | bytes accessed | tf_op | source)
XLA Modules:
  0.0 187.1 jit_solution(17944537122117709830)
XLA Ops:
  0.0 76.7 %shard_map.37 = (bf16[2,64,64,128]{3,2,1,0:T(8,128)(2,1)}, bf16[4,2,8,8,64,128]{5,4,3,2,1,0:T(8,128)(2,1)}) custom-call(bf16[64,128,128]{2,1,0:T(8,128)(2,1)} %map_ref.1), custom_call_target="tpu_custom_call" | custom-call | tf_op jit(solution)/shard_map/pallas_call | solution.py:276
  76.7 0.0 copy-start.1
  76.7 3.0 %copy.6 = f32[2,64,64,128]{3,1,0,2:T(8,128)S(1)} copy(bf16[2,64,64,128]{3,2,1,0:T(8,128)(2,1)} %get-tuple-element.6) | data formatting | bytes 6291456 | tf_op jit(solution)/shard_map/convert_element_type | solution.py:293
  79.6 0.0 copy-done.1
  79.7 0.9 fusion.1
  80.5 0.1 fusion.3
  80.6 4.0 %collective-permute-start = (bf16[14,128,128]{2,1,0:T(8,128)(2,1)S(1)}, bf16[14,128,128]{2,1,0:T(8,128)(2,1)S(1)}, u32[]{:S(2)}, u32[]{:S(2)}) collective-permute-start(bf16[14,128,128]{2,1,0:T(8,128)(2,1)S(1)} %get-tuple-element.9), channel_id=1, source_target_pairs={{0,4},{4,8},{8,12},{12,16},{16,20},{20,24},{24,28},{1,5},{5,9},{9,... | collective-permute-start | bytes 1376264 | tf_op jit(solution)/shard_map/ppermute | solution.py:300
  84.6 0.0 copy-start.4
  84.7 2.4 %collective-permute-start.1 = (bf16[14,128,128]{2,1,0:T(8,128)(2,1)S(1)}, bf16[14,128,128]{2,1,0:T(8,128)(2,1)S(1)}, u32[]{:S(2)}, u32[]{:S(2)}) collective-permute-start(bf16[14,128,128]{2,1,0:T(8,128)(2,1)S(1)} %get-tuple-element.10), channel_id=1, source_target_pairs={{4,0},{8,4},{12,8},{16,12},{20,16},{24,20},{28,24},{5,1},{9,5},{13... | collective-permute-start | bytes 1376264 | tf_op jit(solution)/shard_map/ppermute | solution.py:301
  87.1 6.6 %collective-permute-done = bf16[14,128,128]{2,1,0:T(8,128)(2,1)S(1)} collective-permute-done((bf16[14,128,128]{2,1,0:T(8,128)(2,1)S(1)}, bf16[14,128,128]{2,1,0:T(8,128)(2,1)S(1)}, u32[]{:S(2)}, u32[]{:S(2)}) %collective-permute-start) | collective-permute-done | bytes 458784 | tf_op jit(solution)/shard_map/ppermute | solution.py:300
  93.7 1.2 collective-permute-done.1
  94.9 0.4 pad_maximum_fusion.mid_ref
  95.2 0.0 copy-start
  95.2 1.6 copy-done
  96.8 0.1 fusion.2
  97.0 1.9 %collective-permute-start.2 = (bf16[92,16,128]{2,1,0:T(8,128)(2,1)S(1)}, bf16[92,16,128]{2,1,0:T(8,128)(2,1)S(1)}, u32[]{:S(2)}, u32[]{:S(2)}) collective-permute-start(bf16[92,16,128]{2,1,0:T(8,128)(2,1)S(1)} %get-tuple-element.8), channel_id=1, source_target_pairs={{0,1},{1,2},{2,3},{4,5},{5,6},{6,7},{8,9},{9,10},{10,11},{12,13},{... | collective-permute-start | bytes 1130504 | tf_op jit(solution)/shard_map/ppermute | solution.py:300
  98.9 3.9 %collective-permute-start.3 = (bf16[92,16,128]{2,1,0:T(8,128)(2,1)S(1)}, bf16[92,16,128]{2,1,0:T(8,128)(2,1)S(1)}, u32[]{:S(2)}, u32[]{:S(2)}) collective-permute-start(bf16[92,16,128]{2,1,0:T(8,128)(2,1)S(1)} %get-tuple-element.7), channel_id=1, source_target_pairs={{1,0},{2,1},{3,2},{5,4},{6,5},{7,6},{9,8},{10,9},{11,10},{13,12},{... | collective-permute-start | bytes 1130504 | tf_op jit(solution)/shard_map/ppermute | solution.py:301
  102.8 0.0 copy-done.4
  102.9 0.6 reshape.12.bias_ref
  103.5 0.6 pad_add_fusion.where_ref
  104.1 5.0 %collective-permute-done.2.left_ref = bf16[92,16,128]{2,1,0:T(8,128)(2,1)S(1)} collective-permute-done((bf16[92,16,128]{2,1,0:T(8,128)(2,1)S(1)}, bf16[92,16,128]{2,1,0:T(8,128)(2,1)S(1)}, u32[]{:S(2)}, u32[]{:S(2)}) %collective-permute-start.2) | collective-permute-done | bytes 376864 | tf_op jit(solution)/shard_map/ppermute | solution.py:300
  109.1 0.0 copy-start.2
  109.1 1.9 %collective-permute-done.3.right_ref = bf16[92,16,128]{2,1,0:T(8,128)(2,1)S(1)} collective-permute-done((bf16[92,16,128]{2,1,0:T(8,128)(2,1)S(1)}, bf16[92,16,128]{2,1,0:T(8,128)(2,1)S(1)}, u32[]{:S(2)}, u32[]{:S(2)}) %collective-permute-start.3) | collective-permute-done | bytes 376864 | tf_op jit(solution)/shard_map/ppermute | solution.py:301
  111.1 0.0 copy-start.3
  111.1 0.0 copy-done.2
  111.1 0.7 copy-done.3
  111.8 75.3 %shard_map.38 = bf16[64,128,128]{2,1,0:T(8,128)(2,1)} custom-call(s32[3]{0:T(128)} %pad_add_fusion.where_ref, bf16[92,16,128]{2,1,0:T(8,128)(2,1)} %copy-done.2, bf16[92,128,128]{2,1,0:T(8,128)(2,1)} %copy-done, bf16[92,16,128]{2,1,0:T(8,128)(2,1)} %copy-done.3, bf16[54,128,128]{2,1,0:T(8,128)(2,1)} %bitcast.11, f32[6,1,128]{2,1,0:T(1,128)} %reshape.12.bias_ref), custom_call_target="tpu_custom_call" | custom-call | tf_op jit(solution)/shard_map/pallas_call | solution.py:117
  (1 shorter events, 0.0 us)
Async XLA Ops:
  76.7 3.0 %copy-start.1 = (bf16[64,128,128]{2,1,0:T(8,128)(2,1)S(1)}, bf16[64,128,128]{2,1,0:T(8,128)(2,1)}, u32[]{:S(2)}) copy-start(bf16[64,128,128]{2,1,0:T(8,128)(2,1)} %map_ref.1) | copy-start | bytes 6291460
  80.6 13.1 %collective-permute-start = (bf16[14,128,128]{2,1,0:T(8,128)(2,1)S(1)}, bf16[14,128,128]{2,1,0:T(8,128)(2,1)S(1)}, u32[]{:S(2)}, u32[]{:S(2)}) collective-permute-start(bf16[14,128,128]{2,1,0:T(8,128)(2,1)S(1)} %get-tuple-element.9), channel_id=1, source_target_pairs={{0,4},{4,8},{8,12},{12,16},{16,20},{20,24},{24,28},{1,5},{5,9},{9,... | collective-permute-start | bytes 1376264 | tf_op jit(solution)/shard_map/ppermute | solution.py:300
  84.6 18.2 %copy-start.4 = (f32[2,3,128]{2,0,1:T(2,128)S(1)}, f32[2,3,128]{2,0,1:T(2,128)}, u32[]{:S(2)}) copy-start(f32[2,3,128]{2,0,1:T(2,128)} %param.5) | copy-start | bytes 9220
  84.7 10.2 %collective-permute-start.1 = (bf16[14,128,128]{2,1,0:T(8,128)(2,1)S(1)}, bf16[14,128,128]{2,1,0:T(8,128)(2,1)S(1)}, u32[]{:S(2)}, u32[]{:S(2)}) collective-permute-start(bf16[14,128,128]{2,1,0:T(8,128)(2,1)S(1)} %get-tuple-element.10), channel_id=1, source_target_pairs={{4,0},{8,4},{12,8},{16,12},{20,16},{24,20},{28,24},{5,1},{9,5},{13... | collective-permute-start | bytes 1376264 | tf_op jit(solution)/shard_map/ppermute | solution.py:301
  95.2 1.6 copy-start
  97.0 12.2 %collective-permute-start.2 = (bf16[92,16,128]{2,1,0:T(8,128)(2,1)S(1)}, bf16[92,16,128]{2,1,0:T(8,128)(2,1)S(1)}, u32[]{:S(2)}, u32[]{:S(2)}) collective-permute-start(bf16[92,16,128]{2,1,0:T(8,128)(2,1)S(1)} %get-tuple-element.8), channel_id=1, source_target_pairs={{0,1},{1,2},{2,3},{4,5},{5,6},{6,7},{8,9},{9,10},{10,11},{12,13},{... | collective-permute-start | bytes 1130504 | tf_op jit(solution)/shard_map/ppermute | solution.py:300
  98.9 12.2 %collective-permute-start.3 = (bf16[92,16,128]{2,1,0:T(8,128)(2,1)S(1)}, bf16[92,16,128]{2,1,0:T(8,128)(2,1)S(1)}, u32[]{:S(2)}, u32[]{:S(2)}) collective-permute-start(bf16[92,16,128]{2,1,0:T(8,128)(2,1)S(1)} %get-tuple-element.7), channel_id=1, source_target_pairs={{1,0},{2,1},{3,2},{5,4},{6,5},{7,6},{9,8},{10,9},{11,10},{13,12},{... | collective-permute-start | bytes 1130504 | tf_op jit(solution)/shard_map/ppermute | solution.py:301
  109.1 1.9 %copy-start.2 = (bf16[92,16,128]{2,1,0:T(8,128)(2,1)}, bf16[92,16,128]{2,1,0:T(8,128)(2,1)S(1)}, u32[]{:S(2)}) copy-start(bf16[92,16,128]{2,1,0:T(8,128)(2,1)S(1)} %collective-permute-done.2.left_ref) | copy-start | bytes 1130500
  111.1 0.7 copy-start.3

commit v4 on v3

--- a/solution.py
+++ b/solution.py
@@ -11,9 +11,9 @@
 DILATIONS = (1, 2, 4)
 ROW_HALO = 2 * sum(DILATIONS)
 COL_HALO = 16
-FIRST, PAIRS = 5, 4
+FIRST, PAIRS = 10, 4
 WIDE = ((1, False), (2, False), (1, True), (2, True), (3, False), (4, False), (5, False))
-CHUNKS = 8
+CHUNKS = 16
 MESH = pl.DeviceIdType.MESH
 
 
@@ -94,11 +94,11 @@
         spread(buf_b, row, value, 1)
 
     pairs(buf_b, 0, 2, 2, tall - 2, relu_into(buf_a, 1, 4), PAIRS)
-    pairs(buf_a, 1, 4, 6, tall - 6, first_out, PAIRS)
+    pairs(buf_a, 1, 4, 6, tall - 6, first_out, 8)
     pairs(buf_c, 2, 2, 2, tall - 2, relu_into(buf_a, 1, 4), PAIRS)
-    pairs(buf_a, 3, 4, 6, tall - 6, second_out, PAIRS)
-
-    pairs(buf_b, 4, 1, 8, tall - 8, relu_into(buf_c, 3, 2), 2)
+    pairs(buf_a, 3, 4, 6, tall - 6, second_out, 8)
+
+    pairs(buf_b, 4, 1, 6, tall - 6, relu_into(buf_c, 3, 2), PAIRS)
     pairs(buf_c, 5, 2, 10, tall - 10, relu_into(buf_a, 4, 4), PAIRS)
 
     mid = slice(COL_HALO, COL_HALO + cols)
@@ -107,7 +107,7 @@
         value = mir_ref[row, mid, :].astype(F32) + total + bias_ref[5]
         out_ref[row - ROW_HALO] = value.astype(BF16)
 
-    pairs(buf_a, 6, 4, ROW_HALO, ROW_HALO + rows, last_out, PAIRS, mid)
+    pairs(buf_a, 6, 4, ROW_HALO, ROW_HALO + rows, last_out, 8, mid)
 
 
 def trunk(pieces, where, conv_weight, conv_bias, rows, cols):
@@ -140,7 +140,7 @@
         gap = source - target
         near = ((gap == 1) | (gap == -1)) & (inner_source != inner_target)
         inner = inner_source if via_source else inner_target
-        share = jnp.where(near, inner, k % 2 == 1)
+        share = jnp.where(near, jnp.where(inner, k % 8 != 0, k % 8 == 7), k % 16 in (1, 3, 5, 7, 9, 11, 13))
         return (source != target) & share
 
     def piece(k, f):

time: 189 us -> 180 us (0.952)
  Pallas kernels: 152 us -> 142 us
    pallas_call x1, Pallas kernels: 76.7 us -> 71 us  [exchange(): pl.pallas_call(functools.partial(exchange_kernel, via_source, n_col), out...]
    pallas_call x1, Pallas kernels: 75.3 us -> 71 us  [trunk(): pl.pallas_call(functools.partial(trunk_kernel, rows, cols), out_shape=jax...]
    ppermute x2, waiting for transfers between devices: 3.11 us -> 6.98 us  [halo(): lax.ppermute(lax.slice_in_dim(array, 0, width, axis=dim), axis, down)]
    ppermute x2, waiting for transfers between devices: 11.6 us -> 8.62 us  [halo(): lax.ppermute(lax.slice_in_dim(array, length - width, length, axis=dim), a...]
where the time goes in v4:
time: 180 us
  Pallas kernels  142 us (79%)
  waiting for transfers between devices  15.6 us (9%)
  starting transfers between devices  13.8 us (8%)
  local copies, waits for them, and re-layouts  6.1 us (3%)
  other arithmetic  1.85 us (1%)
    pallas_call x1, Pallas kernels, trunk(): pl.pallas_call(functools.partial(trunk_kernel, rows, cols), out_shape=jax...  71 us
    pallas_call x1, Pallas kernels, exchange(): pl.pallas_call(functools.partial(exchange_kernel, via_source, n_col), out...  71 us
    ppermute x2, waiting for transfers between devices, halo(): lax.ppermute(lax.slice_in_dim(array, length - width, length, axis=dim), a...  8.62 us
    ppermute x2, starting transfers between devices, halo(): lax.ppermute(lax.slice_in_dim(array, length - width, length, axis=dim), a...  7.77 us
    ppermute x2, waiting for transfers between devices, halo(): lax.ppermute(lax.slice_in_dim(array, 0, width, axis=dim), axis, down)  6.98 us
    ppermute x2, starting transfers between devices, halo(): lax.ppermute(lax.slice_in_dim(array, 0, width, axis=dim), axis, down)  6.06 us
  transfers between devices with their start and end apart: 4, of which 4 were waited for; matrix products, arithmetic and copies ran while one was open for 1% of the time, Pallas kernels for 0%

profile of v4, /device:TPU:12, one launch (start us, length us, event | category | flops | bytes accessed | tf_op | source)
XLA Modules:
  0.0 179.5 jit_solution(5888471464264712859)
XLA Ops:
  0.0 71.0 %shard_map.37 = (bf16[2,64,64,128]{3,2,1,0:T(8,128)(2,1)}, bf16[4,2,16,4,64,128]{5,4,3,2,1,0:T(8,128)(2,1)}) custom-call(bf16[64,128,128]{2,1,0:T(8,128)(2,1)} %map_ref.1), custom_call_target="tpu_custom_call" | custom-call | tf_op jit(solution)/shard_map/pallas_call | solution.py:276
  71.0 0.0 copy-start.1
  71.0 3.0 %copy.6 = f32[2,64,64,128]{3,1,0,2:T(8,128)S(1)} copy(bf16[2,64,64,128]{3,2,1,0:T(8,128)(2,1)} %get-tuple-element.6) | data formatting | bytes 6291456 | tf_op jit(solution)/shard_map/convert_element_type | solution.py:293
  74.0 0.0 copy-done.1
  74.0 0.9 fusion.1
  74.9 0.1 fusion.3
  75.0 2.5 %collective-permute-start = (bf16[14,128,128]{2,1,0:T(8,128)(2,1)S(1)}, bf16[14,128,128]{2,1,0:T(8,128)(2,1)S(1)}, u32[]{:S(2)}, u32[]{:S(2)}) collective-permute-start(bf16[14,128,128]{2,1,0:T(8,128)(2,1)S(1)} %get-tuple-element.9), channel_id=1, source_target_pairs={{0,4},{4,8},{8,12},{12,16},{16,20},{20,24},{24,28},{1,5},{5,9},{9,... | collective-permute-start | bytes 1376264 | tf_op jit(solution)/shard_map/ppermute | solution.py:300
  77.5 0.0 copy-start.4
  77.5 4.0 %collective-permute-start.1 = (bf16[14,128,128]{2,1,0:T(8,128)(2,1)S(1)}, bf16[14,128,128]{2,1,0:T(8,128)(2,1)S(1)}, u32[]{:S(2)}, u32[]{:S(2)}) collective-permute-start(bf16[14,128,128]{2,1,0:T(8,128)(2,1)S(1)} %get-tuple-element.10), channel_id=1, source_target_pairs={{4,0},{8,4},{12,8},{16,12},{20,16},{24,20},{28,24},{5,1},{9,5},{13... | collective-permute-start | bytes 1376264 | tf_op jit(solution)/shard_map/ppermute | solution.py:301
  81.4 4.2 %collective-permute-done = bf16[14,128,128]{2,1,0:T(8,128)(2,1)S(1)} collective-permute-done((bf16[14,128,128]{2,1,0:T(8,128)(2,1)S(1)}, bf16[14,128,128]{2,1,0:T(8,128)(2,1)S(1)}, u32[]{:S(2)}, u32[]{:S(2)}) %collective-permute-start) | collective-permute-done | bytes 458784 | tf_op jit(solution)/shard_map/ppermute | solution.py:300
  85.7 2.9 %collective-permute-done.1 = bf16[14,128,128]{2,1,0:T(8,128)(2,1)S(1)} collective-permute-done((bf16[14,128,128]{2,1,0:T(8,128)(2,1)S(1)}, bf16[14,128,128]{2,1,0:T(8,128)(2,1)S(1)}, u32[]{:S(2)}, u32[]{:S(2)}) %collective-permute-start.1) | collective-permute-done | bytes 458784 | tf_op jit(solution)/shard_map/ppermute | solution.py:301
  88.5 0.4 pad_maximum_fusion.mid_ref
  88.9 0.0 copy-start
  88.9 1.6 copy-done
  90.5 0.1 fusion.2
  90.6 5.3 %collective-permute-start.2 = (bf16[92,16,128]{2,1,0:T(8,128)(2,1)S(1)}, bf16[92,16,128]{2,1,0:T(8,128)(2,1)S(1)}, u32[]{:S(2)}, u32[]{:S(2)}) collective-permute-start(bf16[92,16,128]{2,1,0:T(8,128)(2,1)S(1)} %get-tuple-element.8), channel_id=1, source_target_pairs={{0,1},{1,2},{2,3},{4,5},{5,6},{6,7},{8,9},{9,10},{10,11},{12,13},{... | collective-permute-start | bytes 1130504 | tf_op jit(solution)/shard_map/ppermute | solution.py:300
  95.9 2.1 %collective-permute-start.3 = (bf16[92,16,128]{2,1,0:T(8,128)(2,1)S(1)}, bf16[92,16,128]{2,1,0:T(8,128)(2,1)S(1)}, u32[]{:S(2)}, u32[]{:S(2)}) collective-permute-start(bf16[92,16,128]{2,1,0:T(8,128)(2,1)S(1)} %get-tuple-element.7), channel_id=1, source_target_pairs={{1,0},{2,1},{3,2},{5,4},{6,5},{7,6},{9,8},{10,9},{11,10},{13,12},{... | collective-permute-start | bytes 1130504 | tf_op jit(solution)/shard_map/ppermute | solution.py:301
  98.0 0.0 copy-done.4
  98.0 0.6 reshape.12.bias_ref
  98.6 0.6 pad_add_fusion.where_ref
  99.3 4.4 %collective-permute-done.2.left_ref = bf16[92,16,128]{2,1,0:T(8,128)(2,1)S(1)} collective-permute-done((bf16[92,16,128]{2,1,0:T(8,128)(2,1)S(1)}, bf16[92,16,128]{2,1,0:T(8,128)(2,1)S(1)}, u32[]{:S(2)}, u32[]{:S(2)}) %collective-permute-start.2) | collective-permute-done | bytes 376864 | tf_op jit(solution)/shard_map/ppermute | solution.py:300
  103.7 0.0 copy-start.2
  103.7 4.1 %collective-permute-done.3.right_ref = bf16[92,16,128]{2,1,0:T(8,128)(2,1)S(1)} collective-permute-done((bf16[92,16,128]{2,1,0:T(8,128)(2,1)S(1)}, bf16[92,16,128]{2,1,0:T(8,128)(2,1)S(1)}, u32[]{:S(2)}, u32[]{:S(2)}) %collective-permute-start.3) | collective-permute-done | bytes 376864 | tf_op jit(solution)/shard_map/ppermute | solution.py:301
  107.8 0.0 copy-start.3
  107.8 0.0 copy-done.2
  107.8 0.7 copy-done.3
  108.5 71.0 %shard_map.38 = bf16[64,128,128]{2,1,0:T(8,128)(2,1)} custom-call(s32[3]{0:T(128)} %pad_add_fusion.where_ref, bf16[92,16,128]{2,1,0:T(8,128)(2,1)} %copy-done.2, bf16[92,128,128]{2,1,0:T(8,128)(2,1)} %copy-done, bf16[92,16,128]{2,1,0:T(8,128)(2,1)} %copy-done.3, bf16[54,128,128]{2,1,0:T(8,128)(2,1)} %bitcast.11, f32[6,1,128]{2,1,0:T(1,128)} %reshape.12.bias_ref), custom_call_target="tpu_custom_call" | custom-call | tf_op jit(solution)/shard_map/pallas_call | solution.py:117
  (1 shorter events, 0.0 us)
Async XLA Ops:
  71.0 3.0 %copy-start.1 = (bf16[64,128,128]{2,1,0:T(8,128)(2,1)S(1)}, bf16[64,128,128]{2,1,0:T(8,128)(2,1)}, u32[]{:S(2)}) copy-start(bf16[64,128,128]{2,1,0:T(8,128)(2,1)} %map_ref.1) | copy-start | bytes 6291460
  75.0 10.7 %collective-permute-start = (bf16[14,128,128]{2,1,0:T(8,128)(2,1)S(1)}, bf16[14,128,128]{2,1,0:T(8,128)(2,1)S(1)}, u32[]{:S(2)}, u32[]{:S(2)}) collective-permute-start(bf16[14,128,128]{2,1,0:T(8,128)(2,1)S(1)} %get-tuple-element.9), channel_id=1, source_target_pairs={{0,4},{4,8},{8,12},{12,16},{16,20},{20,24},{24,28},{1,5},{5,9},{9,... | collective-permute-start | bytes 1376264 | tf_op jit(solution)/shard_map/ppermute | solution.py:300
  77.5 20.5 %copy-start.4 = (f32[2,3,128]{2,0,1:T(2,128)S(1)}, f32[2,3,128]{2,0,1:T(2,128)}, u32[]{:S(2)}) copy-start(f32[2,3,128]{2,0,1:T(2,128)} %param.5) | copy-start | bytes 9220
  77.5 11.0 %collective-permute-start.1 = (bf16[14,128,128]{2,1,0:T(8,128)(2,1)S(1)}, bf16[14,128,128]{2,1,0:T(8,128)(2,1)S(1)}, u32[]{:S(2)}, u32[]{:S(2)}) collective-permute-start(bf16[14,128,128]{2,1,0:T(8,128)(2,1)S(1)} %get-tuple-element.10), channel_id=1, source_target_pairs={{4,0},{8,4},{12,8},{16,12},{20,16},{24,20},{28,24},{5,1},{9,5},{13... | collective-permute-start | bytes 1376264 | tf_op jit(solution)/shard_map/ppermute | solution.py:301
  88.9 1.6 copy-start
  90.6 13.1 %collective-permute-start.2 = (bf16[92,16,128]{2,1,0:T(8,128)(2,1)S(1)}, bf16[92,16,128]{2,1,0:T(8,128)(2,1)S(1)}, u32[]{:S(2)}, u32[]{:S(2)}) collective-permute-start(bf16[92,16,128]{2,1,0:T(8,128)(2,1)S(1)} %get-tuple-element.8), channel_id=1, source_target_pairs={{0,1},{1,2},{2,3},{4,5},{5,6},{6,7},{8,9},{9,10},{10,11},{12,13},{... | collective-permute-start | bytes 1130504 | tf_op jit(solution)/shard_map/ppermute | solution.py:300
  95.9 11.9 %collective-permute-start.3 = (bf16[92,16,128]{2,1,0:T(8,128)(2,1)S(1)}, bf16[92,16,128]{2,1,0:T(8,128)(2,1)S(1)}, u32[]{:S(2)}, u32[]{:S(2)}) collective-permute-start(bf16[92,16,128]{2,1,0:T(8,128)(2,1)S(1)} %get-tuple-element.7), channel_id=1, source_target_pairs={{1,0},{2,1},{3,2},{5,4},{6,5},{7,6},{9,8},{10,9},{11,10},{13,12},{... | collective-permute-start | bytes 1130504 | tf_op jit(solution)/shard_map/ppermute | solution.py:301
  103.7 4.1 %copy-start.2 = (bf16[92,16,128]{2,1,0:T(8,128)(2,1)}, bf16[92,16,128]{2,1,0:T(8,128)(2,1)S(1)}, u32[]{:S(2)}) copy-start(bf16[92,16,128]{2,1,0:T(8,128)(2,1)S(1)} %collective-permute-done.2.left_ref) | copy-start | bytes 1130500
  107.8 0.7 copy-start.3
